TPU v7x, 1024 devices: a whole 4x8x16 slice. The times are simulated.
1024 devices in a mesh: replica: 16 (over x, z_hi), fsdp: 64 (over y, z_lo, core).
Axes of the slice: x: 4, y: 8, z: 16 (z_hi: 4, z_lo: 4; z = z_hi * 4 + z_lo), core: 2. Of those that a mesh axis runs over, the one named last changes fastest.
Arguments:
- queries: bfloat16 [16, 8192, 2048], P('replica', 'fsdp'), may hold values from -6 to 6, as said below
- key_rows: bfloat16 [16, 8192, 2048], P('replica', 'fsdp'), may hold values from -6 to 6
- value_rows: bfloat16 [16, 8192, 2048], P('replica', 'fsdp'), may hold values from -6 to 6
- cotangent: bfloat16 [16, 20, 8192], P('replica', None, 'fsdp'), may hold values from -6 to 6
- readout: float32 [16, 20, 2048], P('replica', None, 'fsdp'), may hold values from -3 to 3
- rand_blocks: int32 [64, 2], replicated, may hold values from 0 to 63
- global_blocks: int32 [1], replicated, may hold values from 0 to 63
- hyper_dim: int32 [20], replicated, may hold values from 0 to 3
Outputs:
- attention: bfloat16 [16, 8192, 2048], P('replica', 'fsdp')
- new_readout: float32 [16, 20, 2048], P('replica', None, 'fsdp')
Inputs may be any that keep to these rules, and one draw needn't show every extreme that they name: `queries`: queries and keys lie within the range. `rand_blocks`: each entry names a block of the window; it may repeat a window or global block.
All inputs are finite; a program needn't handle non-finite values.
Results may differ from a plain program's by a relative error of at most 0.0049.
Values may be sent and summed in bfloat16 or wider, within the bound.
No kernel may reach another device: no remote copies, remote signals or barrier semaphores. Data moves between devices by JAX's collectives and lax.ppermute only.
A program may use at most 64 MiB of HBM per device.

v0:
```python
import jax
import jax.numpy as jnp
from jax import lax
from jax.sharding import PartitionSpec as P

BLOCK = 128
HEAD_SIZE = 128


LEARN_RATE = 0.01
head_group = 4


def from_partner(value, axis, distance):
    return lax.ppermute(value, axis, [(i, i ^ 1 << distance) for i in range(lax.axis_size(axis))])


def local(queries, key_rows, value_rows, cotangent, readout, rand_blocks, global_blocks, hyper_dim):
    group_count = lax.axis_size("fsdp")
    position = lax.axis_index("fsdp")
    query_rows = queries[0]
    own_keys = key_rows[0]
    own_values = value_rows[0]
    tok_count, width = query_rows.shape
    local_blocks = tok_count // BLOCK
    all_blocks = local_blocks * group_count
    heads = width // HEAD_SIZE
    block_ids = jnp.arange(all_blocks, dtype=jnp.int32)
    far_columns = jnp.concatenate(
        [
            rand_blocks,
            jnp.broadcast_to(global_blocks[None, :], (all_blocks, global_blocks.shape[0])),
        ],
        axis=1,
    )
    key_view = own_keys.reshape(local_blocks, BLOCK, width)
    value_view = own_values.reshape(local_blocks, BLOCK, width)
    held_keys, held_values = (
        lax.all_to_all(key_view, "fsdp", split_axis=1, concat_axis=0, tiled=True),
        lax.all_to_all(value_view, "fsdp", split_axis=1, concat_axis=0, tiled=True),
    )
    wanted = jnp.concatenate(
        [(block_ids - 1)[:, None], (block_ids + 1)[:, None], far_columns], axis=1
    )
    picked = jnp.clip(wanted, 0, all_blocks - 1)
    sent_keys = held_keys[picked]
    sent_values = held_values[picked]
    got_keys, got_values = (
        lax.all_to_all(sent_keys, "fsdp", split_axis=0, concat_axis=2, tiled=True),
        lax.all_to_all(sent_values, "fsdp", split_axis=0, concat_axis=2, tiled=True),
    )
    key_sets = jnp.concatenate([key_view[:, None], got_keys], axis=1)
    value_sets = jnp.concatenate([value_view[:, None], got_values], axis=1)
    own_ids = position * local_blocks + jnp.arange(local_blocks, dtype=jnp.int32)
    always = jnp.ones((local_blocks, far_columns.shape[1] + 1), dtype=bool)
    usable = jnp.concatenate(
        [
            always[:, :1],
            (own_ids >= 1)[:, None],
            (own_ids + 1 < all_blocks)[:, None],
            always[:, 1:],
        ],
        axis=1,
    )
    key_mask = jnp.repeat(usable, BLOCK, axis=1)
    key_flat = key_sets.reshape(local_blocks, -1, heads, HEAD_SIZE)
    value_flat = value_sets.reshape(local_blocks, -1, heads, HEAD_SIZE)
    query_heads = query_rows.reshape(local_blocks, BLOCK, heads, HEAD_SIZE)
    factor = HEAD_SIZE ** (-0.5)

    def attend(offset):
        query_part = lax.dynamic_slice_in_dim(query_heads, offset, head_group, 2)
        key_part = lax.dynamic_slice_in_dim(key_flat, offset, head_group, 2)
        value_part = lax.dynamic_slice_in_dim(value_flat, offset, head_group, 2)
        scores = (
            jnp.einsum("bqhd,bkhd->bhqk", query_part, key_part, preferred_element_type=jnp.float32)
            * factor
        )
        scores = jnp.where(key_mask[:, None, None, :], scores, -jnp.inf)
        row_max = jnp.max(scores, axis=-1, keepdims=True)
        weights = jnp.exp(scores - row_max)
        chances = (weights / jnp.sum(weights, axis=-1, keepdims=True)).astype(jnp.bfloat16)
        mixed = jnp.einsum(
            "bhqk,bkhd->bqhd", chances, value_part, preferred_element_type=jnp.float32
        )
        return mixed.astype(jnp.bfloat16)

    outputs = lax.map(attend, jnp.arange(0, heads, head_group, dtype=jnp.int32))
    attention = jnp.moveaxis(outputs, 0, 2).reshape(tok_count, width)
    term = jnp.dot(cotangent[0], attention, preferred_element_type=jnp.float32)
    grad_share = lax.psum_scatter(term, "fsdp", scatter_dimension=1, tiled=True)
    stepped = readout[0] - LEARN_RATE * grad_share
    levels = lax.axis_size("replica").bit_length() - 1
    blended = stepped
    for bit_index in range(levels):
        partner_rows = from_partner(stepped, "replica", bit_index)
        blended = jnp.where(
            (hyper_dim == bit_index)[:, None], 0.5 * (stepped + partner_rows), blended
        )
    return (attention[None], blended[None])


def solution(mesh):
    placed = (
        P("replica", "fsdp", None),
        P("replica", "fsdp", None),
        P("replica", "fsdp", None),
        P("replica", None, "fsdp"),
        P("replica", None, "fsdp"),
        P(),
        P(),
        P(),
    )
    return jax.shard_map(
        local,
        mesh=mesh,
        in_specs=placed,
        out_specs=(P("replica", "fsdp", None), P("replica", None, "fsdp")),
        check_vma=False,
    )
```

profile of v0, /device:TPU:2, one launch (start us, length us, event | category | flops | bytes accessed | tf_op | source)
XLA Modules:
  0.0 602.9 jit_solution(945668245997156329)
XLA Ops:
  9.6 3.9 reduce.8
  14.7 13.5 %all-to-all-start = ((bf16[64,2,2048]{2,1,0:T(2,128)(2,1)}), bf16[64,2,2048]{2,1,0:T(2,128)(2,1)S(1)}, u32[]{:S(2)}, u32[]{:S(2)}) async-start(bf16[64,2,2048]{2,1,0:T(2,128)(2,1)} %reshape.164), calls=%async_computation | async-start | bytes 1048576 | tf_op jit(solution)/shard_map/all_to_all | solution.py:40
  29.1 3.9 reduce.9
  34.2 12.5 %all-to-all-done = bf16[64,2,2048]{2,1,0:T(2,128)(2,1)S(1)} async-done(((bf16[64,2,2048]{2,1,0:T(2,128)(2,1)}), bf16[64,2,2048]{2,1,0:T(2,128)(2,1)S(1)}, u32[]{:S(2)}, u32[]{:S(2)}) %all-to-all-start) | async-done | bytes 524320 | tf_op jit(solution)/shard_map/all_to_all | solution.py:40
  46.7 5.1 all-to-all-start.2
  56.7 14.5 %gather_fusion = bf16[320,2,2048]{2,1,0:T(2,128)(2,1)} fusion(bf16[64,2,2048]{2,1,0:T(2,128)(2,1)S(1)} %all_to_all.45, s32[1024]{0:T(1024)S(1)} %pad_clamp_fusion), kind=kCustom, calls=%fused_computation | custom fusion | bytes 5244160 | tf_op jit(solution)/shard_map/gather | solution.py:47
  71.3 10.9 %all-to-all-start.1 = ((bf16[64,5,2,2048]{3,2,1,0:T(2,128)(2,1)}), bf16[64,5,2,2048]{3,2,1,0:T(2,128)(2,1)S(1)}, u32[]{:S(2)}, u32[]{:S(2)}) async-start(bf16[64,5,2,2048]{3,2,1,0:T(2,128)(2,1)} %bitcast.119), calls=%async_computation.1 | async-start | bytes 5242880 | tf_op jit(solution)/shard_map/all_to_all | solution.py:50
  84.0 5.0 bitcast_reduce_fusion
  90.5 14.5 %gather_fusion.1 = bf16[320,2,2048]{2,1,0:T(2,128)(2,1)} fusion(bf16[64,2,2048]{2,1,0:T(2,128)(2,1)S(1)} %all_to_all.51, s32[1024]{0:T(1024)S(1)} %pad_clamp_fusion), kind=kCustom, calls=%fused_computation.1 | custom fusion | bytes 5244160 | tf_op jit(solution)/shard_map/gather | solution.py:46
  105.0 41.2 %all-to-all-done.1 = bf16[64,5,2,2048]{3,2,1,0:T(2,128)(2,1)S(1)} async-done(((bf16[64,5,2,2048]{3,2,1,0:T(2,128)(2,1)}), bf16[64,5,2,2048]{3,2,1,0:T(2,128)(2,1)S(1)}, u32[]{:S(2)}, u32[]{:S(2)}) %all-to-all-start.1) | async-done | bytes 2621472 | tf_op jit(solution)/shard_map/all_to_all | solution.py:50
  146.2 6.2 %all-to-all-start.3 = ((bf16[64,5,2,2048]{3,2,1,0:T(2,128)(2,1)}), bf16[64,5,2,2048]{3,2,1,0:T(2,128)(2,1)}, u32[]{:S(2)}, u32[]{:S(2)}) async-start(bf16[64,5,2,2048]{3,2,1,0:T(2,128)(2,1)} %bitcast.118), calls=%async_computation.3 | async-start | bytes 5242880 | tf_op jit(solution)/shard_map/all_to_all | solution.py:49
  153.9 3.6 copy.53
  157.4 3.8 all_to_all.49
  164.2 52.0 %all-to-all-done.3 = bf16[64,5,2,2048]{3,2,1,0:T(2,128)(2,1)} async-done(((bf16[64,5,2,2048]{3,2,1,0:T(2,128)(2,1)}), bf16[64,5,2,2048]{3,2,1,0:T(2,128)(2,1)}, u32[]{:S(2)}, u32[]{:S(2)}) %all-to-all-start.3) | async-done | bytes 2621472 | tf_op jit(solution)/shard_map/all_to_all | solution.py:49
  216.2 3.8 copy.56
  227.8 45.2 %while.11 = (s32[]{:T(128)}, bf16[4,1,128,4,128]{2,4,3,1,0:T(8,128)(2,1)S(1)}, s32[4]{0:T(128)S(1)}, bf16[1,768,16,128]{3,2,1,0:T(8,128)(2,1)}, bf16[1,128,16,12...) while((s32[]{:T(128)}, ...), condition=%wide.region_3.4_spmd.clone, body=%wide.region_0.3_spmd.clone.sunk | while | flops 203752192 | bytes 9705125 | solution.py:88
  230.4 3.9 constant_dynamic-slice_fusion.3
  242.1 3.9 constant_dynamic-slice_fusion.3
  274.8 291.5 %reduce-scatter.4.cloned.1.call-done = f32[32,20]{1,0:T(8,128)} async-done(((f32[2048,20]{1,0:T(8,128)}), f32[32,20]{1,0:T(8,128)}) %reduce-scatter.4.cloned.1.call-update) | async-done | bytes 2576
  567.1 4.0 collective-permute-start
  571.2 3.2 collective-permute-start.1
  574.4 11.0 %collective-permute-start.2 = (f32[20,32]{1,0:T(8,128)S(1)}, f32[20,32]{1,0:T(8,128)S(1)}, u32[]{:S(2)}, u32[]{:S(2)}) collective-permute-start(f32[20,32]{1,0:T(8,128)S(1)} %bitcast_subtract_fusion), channel_id=1, source_target_pairs={{0,128},{64,192},{128,0},{192,64},{256,384},{320,448},{384,256},{4... | collective-permute-start | bytes 7688 | tf_op jit(solution)/shard_map/ppermute | solution.py:15
  585.4 3.2 collective-permute-start.3
  589.7 5.2 collective-permute-done.3
  (80 shorter events, 59.0 us)
Async XLA Ops:
  7.2 265.9 %copy-start = (bf16[1,20,128]{2,1,0:T(8,128)(2,1)S(1)}, bf16[1,20,128]{2,1,0:T(8,128)(2,1)}, u32[]{:S(2)}) copy-start(bf16[1,20,128]{2,1,0:T(8,128)(2,1)} %param.13) | copy-start | bytes 15364
  7.2 21.1 %copy-start.2 = (bf16[1,128,2048]{2,1,0:T(8,128)(2,1)S(1)}, bf16[1,128,2048]{2,1,0:T(8,128)(2,1)}, u32[]{:S(2)}) copy-start(bf16[1,128,2048]{2,1,0:T(8,128)(2,1)} %param.11) | copy-start | bytes 1572868
  14.7 32.0 %all-to-all-start = ((bf16[64,2,2048]{2,1,0:T(2,128)(2,1)}), bf16[64,2,2048]{2,1,0:T(2,128)(2,1)S(1)}, u32[]{:S(2)}, u32[]{:S(2)}) async-start(bf16[64,2,2048]{2,1,0:T(2,128)(2,1)} %reshape.164), calls=%async_computation | async-start | bytes 1048576 | tf_op jit(solution)/shard_map/all_to_all | solution.py:40
  28.3 24.3 %copy-start.7 = (s32[64,2]{0,1:T(2,128)S(1)}, s32[64,2]{0,1:T(2,128)}, u32[]{:S(2)}) copy-start(s32[64,2]{0,1:T(2,128)} %param.15) | copy-start | bytes 1540
  46.7 24.5 %all-to-all-start.2 = ((bf16[64,2,2048]{2,1,0:T(2,128)(2,1)}), bf16[64,2,2048]{2,1,0:T(2,128)(2,1)S(1)}, u32[]{:S(2)}, u32[]{:S(2)}) async-start(bf16[64,2,2048]{2,1,0:T(2,128)(2,1)} %reshape.166), calls=%async_computation.2 | async-start | bytes 1048576 | tf_op jit(solution)/shard_map/all_to_all | solution.py:39
  71.3 74.9 %all-to-all-start.1 = ((bf16[64,5,2,2048]{3,2,1,0:T(2,128)(2,1)}), bf16[64,5,2,2048]{3,2,1,0:T(2,128)(2,1)S(1)}, u32[]{:S(2)}, u32[]{:S(2)}) async-start(bf16[64,5,2,2048]{3,2,1,0:T(2,128)(2,1)} %bitcast.119), calls=%async_computation.1 | async-start | bytes 5242880 | tf_op jit(solution)/shard_map/all_to_all | solution.py:50
  146.2 6.5 %copy-start.5 = (bf16[1,128,2048]{2,1,0:T(8,128)(2,1)S(1)}, bf16[1,128,2048]{2,1,0:T(8,128)(2,1)}, u32[]{:S(2)}) copy-start(bf16[1,128,2048]{2,1,0:T(8,128)(2,1)} %param.10) | copy-start | bytes 1572868
  146.2 70.0 %all-to-all-start.3 = ((bf16[64,5,2,2048]{3,2,1,0:T(2,128)(2,1)}), bf16[64,5,2,2048]{3,2,1,0:T(2,128)(2,1)}, u32[]{:S(2)}, u32[]{:S(2)}) async-start(bf16[64,5,2,2048]{3,2,1,0:T(2,128)(2,1)} %bitcast.118), calls=%async_computation.3 | async-start | bytes 5242880 | tf_op jit(solution)/shard_map/all_to_all | solution.py:49
  152.4 413.9 %reduce-scatter.4.cloned.1.call-start = ((), (), s32[]{:S(2)}) async-start(), calls=%async_computation.5 | async-start | bytes 1064960
  157.4 3.8 copy-start.1
  220.0 3.1 copy-start.3
  225.1 2.7 copy-start.4
  273.0 294.1 %copy-start.6 = (f32[1,20,32]{2,0,1:T(1,128)S(1)}, f32[1,20,32]{2,0,1:T(1,128)}, u32[]{:S(2)}) copy-start(f32[1,20,32]{2,0,1:T(1,128)} %param.14) | copy-start | bytes 7684
  273.0 315.5 %copy-start.8 = (s32[20]{0:T(128)S(1)}, s32[20]{0:T(128)}, u32[]{:S(2)}) copy-start(s32[20]{0:T(128)} %param.17) | copy-start | bytes 244
  567.1 22.5 %collective-permute-start = (f32[20,32]{1,0:T(8,128)S(1)}, f32[20,32]{1,0:T(8,128)S(1)}, u32[]{:S(2)}, u32[]{:S(2)}) collective-permute-start(f32[20,32]{1,0:T(8,128)S(1)} %bitcast_subtract_fusion), channel_id=1, source_target_pairs={{0,512},{64,576},{128,640},{192,704},{256,768},{320,832},{384,896}... | collective-permute-start | bytes 7688 | tf_op jit(solution)/shard_map/ppermute | solution.py:15
  571.2 18.5 %collective-permute-start.1 = (f32[20,32]{1,0:T(8,128)S(1)}, f32[20,32]{1,0:T(8,128)S(1)}, u32[]{:S(2)}, u32[]{:S(2)}) collective-permute-start(f32[20,32]{1,0:T(8,128)S(1)} %bitcast_subtract_fusion), channel_id=1, source_target_pairs={{0,256},{64,320},{128,384},{192,448},{256,0},{320,64},{384,128},{4... | collective-permute-start | bytes 7688 | tf_op jit(solution)/shard_map/ppermute | solution.py:15
  574.4 15.2 %collective-permute-start.2 = (f32[20,32]{1,0:T(8,128)S(1)}, f32[20,32]{1,0:T(8,128)S(1)}, u32[]{:S(2)}, u32[]{:S(2)}) collective-permute-start(f32[20,32]{1,0:T(8,128)S(1)} %bitcast_subtract_fusion), channel_id=1, source_target_pairs={{0,128},{64,192},{128,0},{192,64},{256,384},{320,448},{384,256},{4... | collective-permute-start | bytes 7688 | tf_op jit(solution)/shard_map/ppermute | solution.py:15
  585.4 9.5 %collective-permute-start.3 = (f32[20,32]{1,0:T(8,128)S(1)}, f32[20,32]{1,0:T(8,128)S(1)}, u32[]{:S(2)}, u32[]{:S(2)}) collective-permute-start(f32[20,32]{1,0:T(8,128)S(1)} %bitcast_subtract_fusion), channel_id=1, source_target_pairs={{0,64},{64,0},{128,192},{192,128},{256,320},{320,256},{384,448},{4... | collective-permute-start | bytes 7688 | tf_op jit(solution)/shard_map/ppermute | solution.py:15
Sparse Core Ops, SparseCore 0:
  274.9 291.3 reduce-scatter.3
where the time goes:
time: 612 us; the launch traced here: 603 us
  waiting for transfers between devices  403 us (66%)
  local copies, waits for them, and re-layouts  90.1 us (15%)
  starting transfers between devices  57.4 us (9%)
  matrix products  19 us (3%)
  between operations  15.4 us (3%)
  other arithmetic  10.4 us (2%)
  loops' own time  7.9 us (1%)
    unnamed x2, waiting for transfers between devices  292 us
    all_to_all x1, waiting for transfers between devices, local(): lax.all_to_all(sent_keys, 'fsdp', split_axis=0, concat_axis=2, tiled=True)  52 us
    all_to_all x1, waiting for transfers between devices, local(): lax.all_to_all(sent_values, 'fsdp', split_axis=0, concat_axis=2, tiled=True)  41.2 us
    ppermute x4, starting transfers between devices, from_partner(): lax.ppermute(value, axis, [(i, i ^ 1 << distance) for i in range(lax.axis...  21.4 us
    unnamed x31, local copies, waits for them, and re-layouts  17.1 us
    gather x1, local copies, waits for them, and re-layouts, local(): sent_values = held_values[picked]  14.5 us
    gather x1, local copies, waits for them, and re-layouts, local(): sent_keys = held_keys[picked]  14.5 us
    dynamic_slice x4, local copies, waits for them, and re-layouts, attend(): key_part = lax.dynamic_slice_in_dim(key_flat, offset, head_group, 2)  13.6 us
  transfers between devices with their start and end apart: 9, of which 5 were waited for; matrix products, arithmetic and copies ran while one was open for 9% of the time, Pallas kernels for 0%

commit v1 on v0

v1 whole, which is shorter than its diff:
```python
import functools

import jax
import jax.numpy as jnp
from jax import lax
from jax.experimental import pallas as pl
from jax.experimental.pallas import tpu as pltpu
from jax.sharding import Mesh, PartitionSpec as P

BLOCK = 128
HEAD_SIZE = 128
LEARN_RATE = 0.01
MEMBERS = 4
MEMBER_BITS = 2
LANES = 128
UNROLL = 4
SUBLANES = 8
LOG2_E = 1.4426950408889634


def split_heads(rows_ref, out_ref):
    for head in range(out_ref.shape[0]):
        out_ref[head] = rows_ref[:, head * HEAD_SIZE : (head + 1) * HEAD_SIZE]


def split_queries(query_ref, cot_ref, out_ref):
    heads, rows, _ = out_ref.shape
    joints = cot_ref.shape[0]
    tail = jnp.concatenate(
        [cot_ref[...], jnp.zeros((rows - BLOCK - joints, BLOCK), cot_ref.dtype)], axis=0
    )
    for head in range(heads):
        out_ref[head, :BLOCK, :] = query_ref[:, head * HEAD_SIZE : (head + 1) * HEAD_SIZE]
        out_ref[head, BLOCK:, :] = tail


def join_heads(parts_ref, out_ref):
    for head in range(parts_ref.shape[0]):
        out_ref[:, head * HEAD_SIZE : (head + 1) * HEAD_SIZE] = parts_ref[head]


def attend(
    joints,
    rand_ref,
    global_ref,
    query_ref,
    k0, k1, k2, k3,
    v0, v1, v2, v3,
    readout_ref,
    out_ref,
    own_ref,
    near_ref,
    far_ref,
    cross_ref,
    key_all,
    value_all,
    grad_ref,
    hold_ref,
    sems,
):
    member = lax.axis_index("member")
    per_member = query_ref.shape[0]
    blocks = per_member * MEMBERS
    shard = readout_ref.shape[2]
    per_row = LANES // shard
    part_rows = joints // per_row
    copies = []
    for at, source in enumerate((k0, k1, k2, k3)):
        copies.append(pltpu.make_async_copy(source, key_all.at[at], sems.at[at]))
    for at, source in enumerate((v0, v1, v2, v3)):
        copies.append(pltpu.make_async_copy(source, value_all.at[at], sems.at[MEMBERS + at]))
    for copy in copies:
        copy.start()
    hold_ref[...] = jnp.zeros_like(hold_ref)
    for joint in range(joints):
        hold_ref[joint : joint + 1, :shard] = readout_ref[joint]
    grad_ref[...] = jnp.zeros_like(grad_ref)
    for copy in copies:
        copy.wait()
    factor = (HEAD_SIZE ** (-0.5)) * LOG2_E

    def one_block(at, carry):
        block = at * MEMBERS + member
        listed = [block, jnp.maximum(block - 1, 0), jnp.minimum(block + 1, blocks - 1)]
        listed += [rand_ref[c, block] for c in range(rand_ref.shape[0])]
        listed += [global_ref[c] for c in range(global_ref.shape[0])]
        places = [((b & (MEMBERS - 1)) ^ member, b >> MEMBER_BITS) for b in listed]
        keys = jnp.concatenate([key_all[p, s] for p, s in places], axis=0)
        values = jnp.concatenate([value_all[p, s] for p, s in places], axis=0)
        scores = lax.dot_general(
            query_ref[at, :BLOCK, :],
            keys,
            (((1,), (1,)), ((), ())),
            preferred_element_type=jnp.float32,
        )
        before = jnp.where(block >= 1, 0.0, -jnp.inf).astype(jnp.float32)
        after = jnp.where(block + 1 < blocks, 0.0, -jnp.inf).astype(jnp.float32)
        scores = jnp.concatenate(
            [
                scores[:, :BLOCK],
                scores[:, BLOCK : 2 * BLOCK] + before,
                scores[:, 2 * BLOCK : 3 * BLOCK] + after,
                scores[:, 3 * BLOCK :],
            ],
            axis=1,
        )
        row_max = jnp.max(scores, axis=1, keepdims=True)
        weights = jnp.exp2((scores - row_max) * factor)
        total = jnp.sum(weights, axis=1, keepdims=True)
        chances = (weights * (1.0 / total)).astype(jnp.bfloat16)
        mixed = jnp.dot(chances, values, preferred_element_type=jnp.float32)
        mixed = mixed.astype(jnp.bfloat16)
        out_ref[at] = mixed
        grad_ref[...] += jnp.dot(
            query_ref[at, BLOCK:, :], mixed, preferred_element_type=jnp.float32
        )
        return carry

    lax.fori_loop(0, per_member, one_block, 0, unroll=UNROLL)

    lane = lax.broadcasted_iota(jnp.int32, (SUBLANES, LANES), 1) // shard

    def packed(source_ref, first):
        piece = jnp.zeros((SUBLANES, LANES), jnp.float32)
        for j in range(per_row):
            rows = source_ref[j * part_rows : j * part_rows + SUBLANES, :]
            turn = (j * shard - first) % LANES
            rows = pltpu.roll(rows, turn, 1) if turn else rows
            piece = jnp.where(lane == j, rows, piece)
        return piece

    pieces = [-LEARN_RATE * packed(grad_ref, other * shard) for other in range(MEMBERS)]

    def piece_of(wanted):
        piece = pieces[0]
        for other in range(1, MEMBERS):
            piece = jnp.where(wanted == other, pieces[other], piece)
        return piece

    own_ref[...] = packed(hold_ref, 0) + piece_of(member)
    near_ref[...] = piece_of(member ^ 1)
    far_ref[...] = piece_of(member ^ 2)
    cross_ref[...] = piece_of(member ^ 3)


def blend(joints, hyper_ref, own_ref, *refs):
    partner_refs, out_ref = refs[:-1], refs[-1]
    shard = out_ref.shape[2]
    per_row = LANES // shard
    part_rows = joints // per_row
    lane = lax.broadcasted_iota(jnp.int32, (SUBLANES, LANES), 1) // shard
    row = lax.broadcasted_iota(jnp.int32, (SUBLANES, LANES), 0)
    joint = jnp.where(row < part_rows, lane * part_rows + row, joints)
    dims = jnp.zeros((SUBLANES, LANES), jnp.int32)
    for j in range(joints):
        dims = jnp.where(joint == j, hyper_ref[j], dims)
    own = own_ref[...]
    partner = own
    for bit, ref in enumerate(partner_refs):
        partner = jnp.where(dims == bit, ref[...], partner)
    mixed = 0.5 * (own + partner)
    for j in range(per_row):
        turn = (-j * shard) % LANES
        part = pltpu.roll(mixed, turn, 1) if turn else mixed
        for r in range(part_rows):
            out_ref[j * part_rows + r] = part[r : r + 1, :shard]


def local(queries, key_rows, value_rows, cotangent, readout, rand_blocks, global_blocks, hyper_dim):
    heads = lax.axis_size("head")
    replicas = lax.axis_size("replica")
    joints = cotangent.shape[1]
    shard = readout.shape[2]
    cot_rows = -(-joints // 32) * 32
    vmem = pl.BlockSpec(memory_space=pltpu.VMEM)
    smem = pl.BlockSpec(memory_space=pltpu.SMEM)
    anywhere = pl.BlockSpec(memory_space=pl.ANY)
    by_head = (heads, BLOCK, HEAD_SIZE)

    def spread(value):
        return lax.all_to_all(value, "head", split_axis=0, concat_axis=0, tiled=True)

    def swap(value, distance):
        return lax.ppermute(value, "member", [(i, i ^ distance) for i in range(MEMBERS)])

    def split(rows):
        return pl.pallas_call(
            split_heads,
            out_shape=jax.ShapeDtypeStruct(by_head, rows.dtype),
            in_specs=[vmem],
            out_specs=vmem,
        )(rows)

    split_k = split(key_rows[0])
    k0 = spread(split_k)
    split_v = split(value_rows[0])
    v0 = spread(split_v)
    packed = pl.pallas_call(
        split_queries,
        out_shape=jax.ShapeDtypeStruct((heads, BLOCK + cot_rows, HEAD_SIZE), queries.dtype),
        in_specs=[vmem, vmem],
        out_specs=vmem,
        name="split_queries",
    )(queries[0], cotangent[0])
    q0 = spread(packed)
    k2 = swap(k0, 2)
    k1 = swap(k0, 1)
    k3 = swap(k2, 1)
    v2 = swap(v0, 2)
    v1 = swap(v0, 1)
    v3 = swap(v2, 1)
    piece = jax.ShapeDtypeStruct((SUBLANES, LANES), jnp.float32)
    mixed, own, near, far, cross = pl.pallas_call(
        functools.partial(attend, joints),
        out_shape=(jax.ShapeDtypeStruct(by_head, jnp.bfloat16), piece, piece, piece, piece),
        in_specs=[smem, smem, vmem] + [anywhere] * 8 + [vmem],
        out_specs=(vmem,) * 5,
        scratch_shapes=[
            pltpu.VMEM((MEMBERS, *by_head), jnp.bfloat16),
            pltpu.VMEM((MEMBERS, *by_head), jnp.bfloat16),
            pltpu.VMEM((cot_rows, HEAD_SIZE), jnp.float32),
            pltpu.VMEM((cot_rows, LANES), jnp.float32),
            pltpu.SemaphoreType.DMA((2 * MEMBERS,)),
        ],
        name="attend",
    )(
        rand_blocks.T,
        global_blocks,
        q0,
        k0, k1, k2, k3,
        v0, v1, v2, v3,
        readout.reshape(joints, 1, shard),
    )
    near = swap(near, 1)
    far = swap(far, 2)
    cross = swap(cross, 3)
    returned = spread(mixed)
    stepped = (own + near) + (far + cross)
    partners = []
    for bit in range(replicas.bit_length() - 1):
        partners.append(
            lax.ppermute(
                stepped, "replica", [(i, i ^ 1 << bit) for i in range(replicas)]
            )
        )
    new_readout = pl.pallas_call(
        functools.partial(blend, joints),
        out_shape=jax.ShapeDtypeStruct((joints, 1, shard), jnp.float32),
        in_specs=[smem] + [vmem] * (1 + len(partners)),
        out_specs=vmem,
        name="blend",
    )(hyper_dim, stepped, *partners)
    attention = pl.pallas_call(
        join_heads,
        out_shape=jax.ShapeDtypeStruct((BLOCK, heads * HEAD_SIZE), returned.dtype),
        in_specs=[vmem],
        out_specs=vmem,
        name="join_heads",
    )(returned)
    return (attention[None], new_readout.reshape(1, joints, shard))


def solution(mesh):
    replicas, group = mesh.devices.shape
    fine = Mesh(
        mesh.devices.reshape(replicas, group // MEMBERS, MEMBERS),
        ("replica", "head", "member"),
    )
    rows = P("replica", ("head", "member"), None)
    columns = P("replica", None, ("head", "member"))
    return jax.shard_map(
        local,
        mesh=fine,
        in_specs=(rows, rows, rows, columns, columns, P(), P(), P()),
        out_specs=(rows, columns),
        check_vma=False,
    )
```

time: 612 us -> 168 us (0.27)
  the two profiles are of different devices: /device:TPU:2 before, /device:TPU:8 now
where the time goes in v1:
time: 168 us; the launch traced here: 167 us
  starting transfers between devices  94.6 us (56%)
  waiting for transfers between devices  46.2 us (28%)
  Pallas kernels  22.9 us (14%)
    all_to_all x4, starting transfers between devices, spread(): lax.all_to_all(value, 'head', split_axis=0, concat_axis=0, tiled=True)  38.3 us
    ppermute x4, starting transfers between devices, local(): lax.ppermute(stepped, 'replica', [(i, i ^ 1 << bit) for i in range(replic...  34.1 us
    all_to_all x4, waiting for transfers between devices, spread(): lax.all_to_all(value, 'head', split_axis=0, concat_axis=0, tiled=True)  24.1 us
    ppermute x9, starting transfers between devices, swap(): lax.ppermute(value, 'member', [(i, i ^ distance) for i in range(MEMBERS)])  22.2 us
    ppermute x9, waiting for transfers between devices, swap(): lax.ppermute(value, 'member', [(i, i ^ distance) for i in range(MEMBERS)])  19.9 us
    pallas_call x1, Pallas kernels, local(): pl.pallas_call(functools.partial(attend, joints), out_shape=(jax.ShapeDty...  13.5 us
    pallas_call x2, Pallas kernels, split(): pl.pallas_call(split_heads, out_shape=jax.ShapeDtypeStruct(by_head, rows....  3.89 us
  transfers between devices with their start and end apart: 17, of which 8 were waited for; matrix products, arithmetic and copies ran while one was open for 0% of the time, Pallas kernels for 3%

profile of v1, /device:TPU:8, one launch (start us, length us, event | category | flops | bytes accessed | tf_op | source)
XLA Modules:
  0.0 166.7 jit_solution(8487075768834231438)
XLA Ops:
  0.6 1.9 %shard_map.95 = bf16[16,128,128]{2,1,0:T(8,128)(2,1)} custom-call(bf16[128,2048]{1,0:T(8,128)(2,1)} %bitcast.8), custom_call_target="tpu_custom_call" | custom-call | tf_op jit(solution)/shard_map/pallas_call | solution.py:187
  2.6 16.4 %all-to-all-start.1 = ((bf16[16,128,128]{2,1,0:T(8,128)(2,1)}), bf16[16,128,128]{2,1,0:T(8,128)(2,1)S(1)}, u32[]{:S(2)}, u32[]{:S(2)}) async-start(bf16[16,128,128]{2,1,0:T(8,128)(2,1)} %shard_map.95), calls=%async_computation.1 | async-start | bytes 1048576 | tf_op jit(solution)/shard_map/all_to_all | solution.py:181
  19.0 2.0 %shard_map.96 = bf16[16,128,128]{2,1,0:T(8,128)(2,1)} custom-call(bf16[128,2048]{1,0:T(8,128)(2,1)} %bitcast.9), custom_call_target="tpu_custom_call" | custom-call | tf_op jit(solution)/shard_map/pallas_call | solution.py:187
  21.0 10.1 %all-to-all-done.1.k0 = bf16[16,128,128]{2,1,0:T(8,128)(2,1)S(1)} async-done(((bf16[16,128,128]{2,1,0:T(8,128)(2,1)}), bf16[16,128,128]{2,1,0:T(8,128)(2,1)S(1)}, u32[]{:S(2)}, u32[]{:S(2)}) %all-to-all-start.1) | async-done | bytes 524320 | tf_op jit(solution)/shard_map/all_to_all | solution.py:181
  31.1 4.9 %all-to-all-start.2 = ((bf16[16,128,128]{2,1,0:T(8,128)(2,1)}), bf16[16,128,128]{2,1,0:T(8,128)(2,1)S(1)}, u32[]{:S(2)}, u32[]{:S(2)}) async-start(bf16[16,128,128]{2,1,0:T(8,128)(2,1)} %shard_map.96), calls=%async_computation.2 | async-start | bytes 1048576 | tf_op jit(solution)/shard_map/all_to_all | solution.py:181
  36.0 2.0 %split_queries.1 = bf16[16,160,128]{2,1,0:T(8,128)(2,1)} custom-call(bf16[128,2048]{1,0:T(8,128)(2,1)} %bitcast.10, bf16[20,128]{1,0:T(8,128)(2,1)} %bitcast.14), custom_call_target="tpu_custom_call" | custom-call | tf_op jit(solution)/shard_map/split_queries/pallas_call | solution.py:198
  38.0 13.9 %all-to-all-done.2.v0 = bf16[16,128,128]{2,1,0:T(8,128)(2,1)S(1)} async-done(((bf16[16,128,128]{2,1,0:T(8,128)(2,1)}), bf16[16,128,128]{2,1,0:T(8,128)(2,1)S(1)}, u32[]{:S(2)}, u32[]{:S(2)}) %all-to-all-start.2) | async-done | bytes 524320 | tf_op jit(solution)/shard_map/all_to_all | solution.py:181
  51.9 4.9 %all-to-all-start = ((bf16[16,160,128]{2,1,0:T(8,128)(2,1)}), bf16[16,160,128]{2,1,0:T(8,128)(2,1)S(1)}, u32[]{:S(2)}, u32[]{:S(2)}) async-start(bf16[16,160,128]{2,1,0:T(8,128)(2,1)} %split_queries.1), calls=%async_computation | async-start | bytes 1310720 | tf_op jit(solution)/shard_map/all_to_all | solution.py:181
  56.8 4.3 %collective-permute-start.1 = (bf16[16,128,128]{2,1,0:T(8,128)(2,1)S(1)}, bf16[16,128,128]{2,1,0:T(8,128)(2,1)S(1)}, u32[]{:S(2)}, u32[]{:S(2)}) collective-permute-start(bf16[16,128,128]{2,1,0:T(8,128)(2,1)S(1)} %all-to-all-done.1.k0), channel_id=1, source_target_pairs={{0,2},{1,3},{2,0},{3,1},{4,6},{5,7},{6,4},{7,5},{8,10},{9,11},{10,... | collective-permute-start | bytes 1572872 | tf_op jit(solution)/shard_map/ppermute | solution.py:184
  61.1 1.9 %collective-permute-start.4 = (bf16[16,128,128]{2,1,0:T(8,128)(2,1)S(1)}, bf16[16,128,128]{2,1,0:T(8,128)(2,1)S(1)}, u32[]{:S(2)}, u32[]{:S(2)}) collective-permute-start(bf16[16,128,128]{2,1,0:T(8,128)(2,1)S(1)} %all-to-all-done.2.v0), channel_id=1, source_target_pairs={{0,2},{1,3},{2,0},{3,1},{4,6},{5,7},{6,4},{7,5},{8,10},{9,11},{10,... | collective-permute-start | bytes 1572872 | tf_op jit(solution)/shard_map/ppermute | solution.py:184
  63.0 1.9 %collective-permute-start = (bf16[16,128,128]{2,1,0:T(8,128)(2,1)S(1)}, bf16[16,128,128]{2,1,0:T(8,128)(2,1)S(1)}, u32[]{:S(2)}, u32[]{:S(2)}) collective-permute-start(bf16[16,128,128]{2,1,0:T(8,128)(2,1)S(1)} %all-to-all-done.1.k0), channel_id=1, source_target_pairs={{0,1},{1,0},{2,3},{3,2},{4,5},{5,4},{6,7},{7,6},{8,9},{9,8},{10,11... | collective-permute-start | bytes 1572872 | tf_op jit(solution)/shard_map/ppermute | solution.py:184
  65.0 2.4 %collective-permute-start.3 = (bf16[16,128,128]{2,1,0:T(8,128)(2,1)S(1)}, bf16[16,128,128]{2,1,0:T(8,128)(2,1)}, u32[]{:S(2)}, u32[]{:S(2)}) collective-permute-start(bf16[16,128,128]{2,1,0:T(8,128)(2,1)S(1)} %all-to-all-done.2.v0), channel_id=1, source_target_pairs={{0,1},{1,0},{2,3},{3,2},{4,5},{5,4},{6,7},{7,6},{8,9},{9,8},{10,11... | collective-permute-start | bytes 1572872 | tf_op jit(solution)/shard_map/ppermute | solution.py:184
  67.4 9.4 %collective-permute-done.1.k2 = bf16[16,128,128]{2,1,0:T(8,128)(2,1)S(1)} collective-permute-done((bf16[16,128,128]{2,1,0:T(8,128)(2,1)S(1)}, bf16[16,128,128]{2,1,0:T(8,128)(2,1)S(1)}, u32[]{:S(2)}, u32[]{:S(2)}) %collective-permute-start.1) | collective-permute-done | bytes 524320 | tf_op jit(solution)/shard_map/ppermute | solution.py:184
  78.7 8.2 %collective-permute-done.4.v2 = bf16[16,128,128]{2,1,0:T(8,128)(2,1)S(1)} collective-permute-done((bf16[16,128,128]{2,1,0:T(8,128)(2,1)S(1)}, bf16[16,128,128]{2,1,0:T(8,128)(2,1)S(1)}, u32[]{:S(2)}, u32[]{:S(2)}) %collective-permute-start.4) | collective-permute-done | bytes 524320 | tf_op jit(solution)/shard_map/ppermute | solution.py:184
  90.9 13.5 %attend.1 = (bf16[16,128,128]{2,1,0:T(8,128)(2,1)}, f32[8,128]{1,0:T(8,128)}, f32[8,128]{1,0:T(8,128)}, f32[8,128]{1,0:T(8,128)}, f32[8,128]{1,0:T(8,128)}) custom-call(s32[2,64]{1,0:T(2,128)} %bitcast.15, s32[1]{0:T(128)S(6)} %copy.10.global_ref, bf16[16,160,128]{2,1,0:T(8,128)(2,1)} %copy-done, bf16[16,128,128]{2,1,0:T(8,128)(2,1)} %copy-done.2, ...), custom_call_target="tpu_custom_call" | custom-call | tf_op jit(solution)/shard_map/attend/pallas_call | solution.py:213
  104.4 12.1 %all-to-all-start.3 = ((bf16[16,128,128]{2,1,0:T(8,128)(2,1)}), bf16[16,128,128]{2,1,0:T(8,128)(2,1)S(1)}, u32[]{:S(2)}, u32[]{:S(2)}) async-start(bf16[16,128,128]{2,1,0:T(8,128)(2,1)} %get-tuple-element.7), calls=%async_computation.3 | async-start | bytes 1048576 | tf_op jit(solution)/shard_map/all_to_all | solution.py:181
  116.5 3.9 %collective-permute-start.7 = (f32[8,128]{1,0:T(8,128)S(1)}, f32[8,128]{1,0:T(8,128)S(1)}, u32[]{:S(2)}, u32[]{:S(2)}) collective-permute-start(f32[8,128]{1,0:T(8,128)S(1)} %copy-done.15), channel_id=1, source_target_pairs={{0,2},{1,3},{2,0},{3,1},{4,6},{5,7},{6,4},{7,5},{8,10},{9,11},{10,... | collective-permute-start | bytes 12296 | tf_op jit(solution)/shard_map/ppermute | solution.py:184
  122.3 2.1 %collective-permute-start.6 = (f32[8,128]{1,0:T(8,128)S(1)}, f32[8,128]{1,0:T(8,128)S(1)}, u32[]{:S(2)}, u32[]{:S(2)}) collective-permute-start(f32[8,128]{1,0:T(8,128)S(1)} %copy-done.13), channel_id=1, source_target_pairs={{0,1},{1,0},{2,3},{3,2},{4,5},{5,4},{6,7},{7,6},{8,9},{9,8},{10,11... | collective-permute-start | bytes 12296 | tf_op jit(solution)/shard_map/ppermute | solution.py:184
  125.4 12.9 %collective-permute-start.9 = (f32[8,128]{1,0:T(8,128)S(1)}, f32[8,128]{1,0:T(8,128)S(1)}, u32[]{:S(2)}, u32[]{:S(2)}) collective-permute-start(f32[8,128]{1,0:T(8,128)S(1)} %add_add_fusion.own_ref), channel_id=1, source_target_pairs={{0,64},{64,0},{128,192},{192,128},{256,320},{320,256},{384,448},{4... | collective-permute-start | bytes 12296 | tf_op jit(solution)/shard_map/ppermute | solution.py:242
  138.3 13.1 %collective-permute-start.10 = (f32[8,128]{1,0:T(8,128)S(1)}, f32[8,128]{1,0:T(8,128)S(1)}, u32[]{:S(2)}, u32[]{:S(2)}) collective-permute-start(f32[8,128]{1,0:T(8,128)S(1)} %add_add_fusion.own_ref), channel_id=1, source_target_pairs={{0,128},{64,192},{128,0},{192,64},{256,384},{320,448},{384,256},{4... | collective-permute-start | bytes 12296 | tf_op jit(solution)/shard_map/ppermute | solution.py:242
  151.4 3.4 %collective-permute-start.11 = (f32[8,128]{1,0:T(8,128)S(1)}, f32[8,128]{1,0:T(8,128)S(1)}, u32[]{:S(2)}, u32[]{:S(2)}) collective-permute-start(f32[8,128]{1,0:T(8,128)S(1)} %add_add_fusion.own_ref), channel_id=1, source_target_pairs={{0,256},{64,320},{128,384},{192,448},{256,0},{320,64},{384,128},{4... | collective-permute-start | bytes 12296 | tf_op jit(solution)/shard_map/ppermute | solution.py:242
  154.8 4.7 %collective-permute-start.12 = (f32[8,128]{1,0:T(8,128)S(1)}, f32[8,128]{1,0:T(8,128)S(1)}, u32[]{:S(2)}, u32[]{:S(2)}) collective-permute-start(f32[8,128]{1,0:T(8,128)S(1)} %add_add_fusion.own_ref), channel_id=1, source_target_pairs={{0,512},{64,576},{128,640},{192,704},{256,768},{320,832},{384,896}... | collective-permute-start | bytes 12296 | tf_op jit(solution)/shard_map/ppermute | solution.py:242
  159.6 2.3 %collective-permute-done.12.refs_3_ = f32[8,128]{1,0:T(8,128)S(1)} collective-permute-done((f32[8,128]{1,0:T(8,128)S(1)}, f32[8,128]{1,0:T(8,128)S(1)}, u32[]{:S(2)}, u32[]{:S(2)}) %collective-permute-start.12) | collective-permute-done | bytes 4128 | tf_op jit(solution)/shard_map/ppermute | solution.py:242
  164.7 2.0 %join_heads.1 = bf16[128,2048]{1,0:T(8,128)(2,1)} custom-call(bf16[16,128,128]{2,1,0:T(8,128)(2,1)} %copy-done.1), custom_call_target="tpu_custom_call" | custom-call | tf_op jit(solution)/shard_map/join_heads/pallas_call | solution.py:253
  (49 shorter events, 11.0 us)
Async XLA Ops:
  2.6 28.5 %all-to-all-start.1 = ((bf16[16,128,128]{2,1,0:T(8,128)(2,1)}), bf16[16,128,128]{2,1,0:T(8,128)(2,1)S(1)}, u32[]{:S(2)}, u32[]{:S(2)}) async-start(bf16[16,128,128]{2,1,0:T(8,128)(2,1)} %shard_map.95), calls=%async_computation.1 | async-start | bytes 1048576 | tf_op jit(solution)/shard_map/all_to_all | solution.py:181
  31.1 31.9 %copy-start.2 = (bf16[16,128,128]{2,1,0:T(8,128)(2,1)}, bf16[16,128,128]{2,1,0:T(8,128)(2,1)S(1)}, u32[]{:S(2)}) copy-start(bf16[16,128,128]{2,1,0:T(8,128)(2,1)S(1)} %all-to-all-done.1.k0) | copy-start | bytes 1572868
  31.1 20.9 %all-to-all-start.2 = ((bf16[16,128,128]{2,1,0:T(8,128)(2,1)}), bf16[16,128,128]{2,1,0:T(8,128)(2,1)S(1)}, u32[]{:S(2)}, u32[]{:S(2)}) async-start(bf16[16,128,128]{2,1,0:T(8,128)(2,1)} %shard_map.96), calls=%async_computation.2 | async-start | bytes 1048576 | tf_op jit(solution)/shard_map/all_to_all | solution.py:181
  51.9 13.0 %copy-start.3 = (bf16[16,128,128]{2,1,0:T(8,128)(2,1)}, bf16[16,128,128]{2,1,0:T(8,128)(2,1)S(1)}, u32[]{:S(2)}) copy-start(bf16[16,128,128]{2,1,0:T(8,128)(2,1)S(1)} %all-to-all-done.2.v0) | copy-start | bytes 1572868
  51.9 37.5 %all-to-all-start = ((bf16[16,160,128]{2,1,0:T(8,128)(2,1)}), bf16[16,160,128]{2,1,0:T(8,128)(2,1)S(1)}, u32[]{:S(2)}, u32[]{:S(2)}) async-start(bf16[16,160,128]{2,1,0:T(8,128)(2,1)} %split_queries.1), calls=%async_computation | async-start | bytes 1310720 | tf_op jit(solution)/shard_map/all_to_all | solution.py:181
  56.8 20.0 %collective-permute-start.1 = (bf16[16,128,128]{2,1,0:T(8,128)(2,1)S(1)}, bf16[16,128,128]{2,1,0:T(8,128)(2,1)S(1)}, u32[]{:S(2)}, u32[]{:S(2)}) collective-permute-start(bf16[16,128,128]{2,1,0:T(8,128)(2,1)S(1)} %all-to-all-done.1.k0), channel_id=1, source_target_pairs={{0,2},{1,3},{2,0},{3,1},{4,6},{5,7},{6,4},{7,5},{8,10},{9,11},{10,... | collective-permute-start | bytes 1572872 | tf_op jit(solution)/shard_map/ppermute | solution.py:184
  61.1 25.8 %collective-permute-start.4 = (bf16[16,128,128]{2,1,0:T(8,128)(2,1)S(1)}, bf16[16,128,128]{2,1,0:T(8,128)(2,1)S(1)}, u32[]{:S(2)}, u32[]{:S(2)}) collective-permute-start(bf16[16,128,128]{2,1,0:T(8,128)(2,1)S(1)} %all-to-all-done.2.v0), channel_id=1, source_target_pairs={{0,2},{1,3},{2,0},{3,1},{4,6},{5,7},{6,4},{7,5},{8,10},{9,11},{10,... | collective-permute-start | bytes 1572872 | tf_op jit(solution)/shard_map/ppermute | solution.py:184
  63.0 26.5 %collective-permute-start = (bf16[16,128,128]{2,1,0:T(8,128)(2,1)S(1)}, bf16[16,128,128]{2,1,0:T(8,128)(2,1)S(1)}, u32[]{:S(2)}, u32[]{:S(2)}) collective-permute-start(bf16[16,128,128]{2,1,0:T(8,128)(2,1)S(1)} %all-to-all-done.1.k0), channel_id=1, source_target_pairs={{0,1},{1,0},{2,3},{3,2},{4,5},{5,4},{6,7},{7,6},{8,9},{9,8},{10,11... | collective-permute-start | bytes 1572872 | tf_op jit(solution)/shard_map/ppermute | solution.py:184
  65.0 24.6 %collective-permute-start.3 = (bf16[16,128,128]{2,1,0:T(8,128)(2,1)S(1)}, bf16[16,128,128]{2,1,0:T(8,128)(2,1)}, u32[]{:S(2)}, u32[]{:S(2)}) collective-permute-start(bf16[16,128,128]{2,1,0:T(8,128)(2,1)S(1)} %all-to-all-done.2.v0), channel_id=1, source_target_pairs={{0,1},{1,0},{2,3},{3,2},{4,5},{5,4},{6,7},{7,6},{8,9},{9,8},{10,11... | collective-permute-start | bytes 1572872 | tf_op jit(solution)/shard_map/ppermute | solution.py:184
  76.8 14.1 %copy-start.4 = (bf16[16,128,128]{2,1,0:T(8,128)(2,1)}, bf16[16,128,128]{2,1,0:T(8,128)(2,1)S(1)}, u32[]{:S(2)}) copy-start(bf16[16,128,128]{2,1,0:T(8,128)(2,1)S(1)} %collective-permute-done.1.k2) | copy-start | bytes 1572868
  76.8 12.8 %collective-permute-start.2 = (bf16[16,128,128]{2,1,0:T(8,128)(2,1)S(1)}, bf16[16,128,128]{2,1,0:T(8,128)(2,1)}, u32[]{:S(2)}, u32[]{:S(2)}) collective-permute-start(bf16[16,128,128]{2,1,0:T(8,128)(2,1)S(1)} %collective-permute-done.1.k2), channel_id=1, source_target_pairs={{0,1},{1,0},{2,3},{3,2},{4,5},{5,4},{6,7},{7,6},{8,9},{9,8},{10,11... | collective-permute-start | bytes 1572872 | tf_op jit(solution)/shard_map/ppermute | solution.py:184
  86.9 3.9 %collective-permute-start.5 = (bf16[16,128,128]{2,1,0:T(8,128)(2,1)S(1)}, bf16[16,128,128]{2,1,0:T(8,128)(2,1)}, u32[]{:S(2)}, u32[]{:S(2)}) collective-permute-start(bf16[16,128,128]{2,1,0:T(8,128)(2,1)S(1)} %collective-permute-done.4.v2), channel_id=1, source_target_pairs={{0,1},{1,0},{2,3},{3,2},{4,5},{5,4},{6,7},{7,6},{8,9},{9,8},{10,11... | collective-permute-start | bytes 1572872 | tf_op jit(solution)/shard_map/ppermute | solution.py:184
  104.4 12.1 %copy-start.15 = (f32[8,128]{1,0:T(8,128)S(1)}, f32[8,128]{1,0:T(8,128)}, u32[]{:S(2)}) copy-start(f32[8,128]{1,0:T(8,128)} %get-tuple-element.10) | copy-start | bytes 12292
  104.4 16.0 %copy-start.14 = (f32[8,128]{1,0:T(8,128)S(1)}, f32[8,128]{1,0:T(8,128)}, u32[]{:S(2)}) copy-start(f32[8,128]{1,0:T(8,128)} %get-tuple-element.11) | copy-start | bytes 12292
  104.4 17.9 %copy-start.13 = (f32[8,128]{1,0:T(8,128)S(1)}, f32[8,128]{1,0:T(8,128)}, u32[]{:S(2)}) copy-start(f32[8,128]{1,0:T(8,128)} %get-tuple-element.9) | copy-start | bytes 12292
  104.4 59.6 %all-to-all-start.3 = ((bf16[16,128,128]{2,1,0:T(8,128)(2,1)}), bf16[16,128,128]{2,1,0:T(8,128)(2,1)S(1)}, u32[]{:S(2)}, u32[]{:S(2)}) async-start(bf16[16,128,128]{2,1,0:T(8,128)(2,1)} %get-tuple-element.7), calls=%async_computation.3 | async-start | bytes 1048576 | tf_op jit(solution)/shard_map/all_to_all | solution.py:181
  116.5 7.9 %collective-permute-start.7 = (f32[8,128]{1,0:T(8,128)S(1)}, f32[8,128]{1,0:T(8,128)S(1)}, u32[]{:S(2)}, u32[]{:S(2)}) collective-permute-start(f32[8,128]{1,0:T(8,128)S(1)} %copy-done.15), channel_id=1, source_target_pairs={{0,2},{1,3},{2,0},{3,1},{4,6},{5,7},{6,4},{7,5},{8,10},{9,11},{10,... | collective-permute-start | bytes 12296 | tf_op jit(solution)/shard_map/ppermute | solution.py:184
  120.4 4.9 %collective-permute-start.8 = (f32[8,128]{1,0:T(8,128)S(1)}, f32[8,128]{1,0:T(8,128)S(1)}, u32[]{:S(2)}, u32[]{:S(2)}) collective-permute-start(f32[8,128]{1,0:T(8,128)S(1)} %copy-done.14), channel_id=1, source_target_pairs={{0,3},{1,2},{2,1},{3,0},{4,7},{5,6},{6,5},{7,4},{8,11},{9,10},{10,... | collective-permute-start | bytes 12296 | tf_op jit(solution)/shard_map/ppermute | solution.py:184
  122.3 3.1 %collective-permute-start.6 = (f32[8,128]{1,0:T(8,128)S(1)}, f32[8,128]{1,0:T(8,128)S(1)}, u32[]{:S(2)}, u32[]{:S(2)}) collective-permute-start(f32[8,128]{1,0:T(8,128)S(1)} %copy-done.13), channel_id=1, source_target_pairs={{0,1},{1,0},{2,3},{3,2},{4,5},{5,4},{6,7},{7,6},{8,9},{9,8},{10,11... | collective-permute-start | bytes 12296 | tf_op jit(solution)/shard_map/ppermute | solution.py:184
  125.4 36.5 %copy-start.7 = (f32[8,128]{1,0:T(8,128)}, f32[8,128]{1,0:T(8,128)S(1)}, u32[]{:S(2)}) copy-start(f32[8,128]{1,0:T(8,128)S(1)} %add_add_fusion.own_ref) | copy-start | bytes 12292
  125.4 34.1 %collective-permute-start.9 = (f32[8,128]{1,0:T(8,128)S(1)}, f32[8,128]{1,0:T(8,128)S(1)}, u32[]{:S(2)}, u32[]{:S(2)}) collective-permute-start(f32[8,128]{1,0:T(8,128)S(1)} %add_add_fusion.own_ref), channel_id=1, source_target_pairs={{0,64},{64,0},{128,192},{192,128},{256,320},{320,256},{384,448},{4... | collective-permute-start | bytes 12296 | tf_op jit(solution)/shard_map/ppermute | solution.py:242
  138.3 21.2 %collective-permute-start.10 = (f32[8,128]{1,0:T(8,128)S(1)}, f32[8,128]{1,0:T(8,128)S(1)}, u32[]{:S(2)}, u32[]{:S(2)}) collective-permute-start(f32[8,128]{1,0:T(8,128)S(1)} %add_add_fusion.own_ref), channel_id=1, source_target_pairs={{0,128},{64,192},{128,0},{192,64},{256,384},{320,448},{384,256},{4... | collective-permute-start | bytes 12296 | tf_op jit(solution)/shard_map/ppermute | solution.py:242
  151.4 8.1 %collective-permute-start.11 = (f32[8,128]{1,0:T(8,128)S(1)}, f32[8,128]{1,0:T(8,128)S(1)}, u32[]{:S(2)}, u32[]{:S(2)}) collective-permute-start(f32[8,128]{1,0:T(8,128)S(1)} %add_add_fusion.own_ref), channel_id=1, source_target_pairs={{0,256},{64,320},{128,384},{192,448},{256,0},{320,64},{384,128},{4... | collective-permute-start | bytes 12296 | tf_op jit(solution)/shard_map/ppermute | solution.py:242
  154.8 7.0 %collective-permute-start.12 = (f32[8,128]{1,0:T(8,128)S(1)}, f32[8,128]{1,0:T(8,128)S(1)}, u32[]{:S(2)}, u32[]{:S(2)}) collective-permute-start(f32[8,128]{1,0:T(8,128)S(1)} %add_add_fusion.own_ref), channel_id=1, source_target_pairs={{0,512},{64,576},{128,640},{192,704},{256,768},{320,832},{384,896}... | collective-permute-start | bytes 12296 | tf_op jit(solution)/shard_map/ppermute | solution.py:242
  (9 other events, 23.9 us)

commit v2 on v1

v2 whole, which is shorter than its diff:
```python
import functools

import jax
import jax.numpy as jnp
from jax import lax
from jax.experimental import pallas as pl
from jax.experimental.pallas import tpu as pltpu
from jax.sharding import Mesh, PartitionSpec as P

BLOCK = 128
HEAD_SIZE = 128
LEARN_RATE = 0.01
MEMBERS = 4
MEMBER_BITS = 2
LANES = 128
VMEM_LIMIT = 20 << 20
UNROLL = True
ROW_TILE = 32
SUBLANES = 8
LOG2_E = 1.4426950408889634


def split_heads(rows_ref, out_ref):
    for head in range(out_ref.shape[0]):
        out_ref[head] = rows_ref[:, head * HEAD_SIZE : (head + 1) * HEAD_SIZE]


def split_queries(query_ref, cot_ref, out_ref):
    heads, rows, _ = out_ref.shape
    joints = cot_ref.shape[0]
    tail = jnp.concatenate(
        [cot_ref[...], jnp.zeros((rows - BLOCK - joints, BLOCK), cot_ref.dtype)], axis=0
    )
    for head in range(heads):
        out_ref[head, :BLOCK, :] = query_ref[:, head * HEAD_SIZE : (head + 1) * HEAD_SIZE]
        out_ref[head, BLOCK:, :] = tail


def join_heads(parts_ref, out_ref):
    for head in range(parts_ref.shape[0]):
        out_ref[:, head * HEAD_SIZE : (head + 1) * HEAD_SIZE] = parts_ref[head]


def attend(
    joints,
    rand_ref,
    global_ref,
    query_ref,
    k0, k1, k2, k3,
    v0, v1, v2, v3,
    readout_ref,
    out_ref,
    sent_ref,
    key_all,
    value_all,
    grad_ref,
    hold_ref,
    s_even,
    s_odd,
    p_even,
    p_odd,
    sems,
):
    member = lax.axis_index("member")
    per_member = query_ref.shape[0]
    blocks = per_member * MEMBERS
    shard = readout_ref.shape[2]
    per_row = LANES // shard
    part_rows = joints // per_row
    early = ((k0, key_all.at[0]), (k1, key_all.at[1]), (k2, key_all.at[2]), (v0, value_all.at[0]))
    copies = [pltpu.make_async_copy(*pair, sems.at[at]) for at, pair in enumerate(early)]
    for copy in copies:
        copy.start()
    key_all[3] = k3[...]
    for at, source in ((1, v1), (2, v2), (3, v3)):
        value_all[at] = source[...]
    hold_ref[...] = jnp.zeros_like(hold_ref)
    for joint in range(joints):
        hold_ref[joint : joint + 1, :shard] = readout_ref[joint]
    for copy in copies:
        copy.wait()
    factor = (HEAD_SIZE ** (-0.5)) * LOG2_E

    def listed(at):
        block = at * MEMBERS + member
        ids = [block, jnp.maximum(block - 1, 0), jnp.minimum(block + 1, blocks - 1)]
        ids += [rand_ref[c, block] for c in range(rand_ref.shape[0])]
        ids += [global_ref[c] for c in range(global_ref.shape[0])]
        return block, [((b & (MEMBERS - 1)) ^ member, b >> MEMBER_BITS) for b in ids]

    def score(at, into):
        block, places = listed(at)
        keys = jnp.concatenate([key_all[p, s] for p, s in places], axis=0)
        scores = lax.dot_general(
            query_ref[at, :BLOCK, :],
            keys,
            (((1,), (1,)), ((), ())),
            preferred_element_type=jnp.float32,
        )
        before = jnp.where(block >= 1, 0.0, -jnp.inf).astype(jnp.float32)
        after = jnp.where(block + 1 < blocks, 0.0, -jnp.inf).astype(jnp.float32)
        into[:, :BLOCK] = scores[:, :BLOCK]
        into[:, BLOCK : 2 * BLOCK] = scores[:, BLOCK : 2 * BLOCK] + before
        into[:, 2 * BLOCK : 3 * BLOCK] = scores[:, 2 * BLOCK : 3 * BLOCK] + after
        into[:, 3 * BLOCK :] = scores[:, 3 * BLOCK :]

    def soften(source, into):
        for row in range(0, BLOCK, ROW_TILE):
            rows = slice(row, row + ROW_TILE)
            scores = source[rows, :]
            row_max = jnp.max(scores, axis=1, keepdims=True)
            weights = jnp.exp2((scores - row_max) * factor)
            total = jnp.sum(weights, axis=1, keepdims=True)
            into[rows, :] = (weights * (1.0 / total)).astype(jnp.bfloat16)

    def mix(at, source):
        _, places = listed(at)
        values = jnp.concatenate([value_all[p, s] for p, s in places], axis=0)
        mixed = jnp.dot(source[...], values, preferred_element_type=jnp.float32)
        out_ref[at] = mixed.astype(jnp.bfloat16)

    score(0, s_even)
    score(1, s_odd)
    soften(s_even, p_even)

    def two_blocks(step, carry):
        at = 2 * step
        score(at + 2, s_even)
        soften(s_odd, p_odd)
        mix(at, p_even)
        score(at + 3, s_odd)
        soften(s_even, p_even)
        mix(at + 1, p_odd)
        return carry

    lax.fori_loop(0, per_member // 2 - 1, two_blocks, 0, unroll=UNROLL)
    soften(s_odd, p_odd)
    mix(per_member - 2, p_even)
    mix(per_member - 1, p_odd)
    cots = jnp.concatenate([query_ref[at, BLOCK:, :] for at in range(per_member)], axis=1)
    grad_ref[...] = jnp.dot(
        cots,
        out_ref[...].reshape(per_member * BLOCK, HEAD_SIZE),
        preferred_element_type=jnp.float32,
    )

    lane = lax.broadcasted_iota(jnp.int32, (SUBLANES, LANES), 1) // shard

    def packed(source_ref, first):
        piece = jnp.zeros((SUBLANES, LANES), jnp.float32)
        for j in range(per_row):
            rows = source_ref[j * part_rows : j * part_rows + SUBLANES, :]
            turn = (j * shard - first) % LANES
            rows = pltpu.roll(rows, turn, 1) if turn else rows
            piece = jnp.where(lane == j, rows, piece)
        return piece

    own = packed(hold_ref, 0)
    for other in range(MEMBERS):
        piece = -LEARN_RATE * packed(grad_ref, other * shard)
        piece = piece + jnp.where(other == member, own, 0.0)
        for place in range(sent_ref.shape[0] // MEMBERS):
            sent_ref[place * MEMBERS + other] = piece


def stepped_of(got_ref, place):
    rows = [got_ref[place * MEMBERS + m] for m in range(MEMBERS)]
    return functools.reduce(jnp.add, rows)


def own_step(got_ref, out_ref):
    out_ref[...] = stepped_of(got_ref, lax.axis_index("upper"))


def blend(joints, hyper_ref, got_ref, own_ref, *refs):
    lower_refs, out_ref = refs[:-1], refs[-1]
    upper = lax.axis_index("upper")
    upper_bits = (got_ref.shape[0] // MEMBERS).bit_length() - 1
    shard = out_ref.shape[2]
    per_row = LANES // shard
    part_rows = joints // per_row
    lane = lax.broadcasted_iota(jnp.int32, (SUBLANES, LANES), 1) // shard
    row = lax.broadcasted_iota(jnp.int32, (SUBLANES, LANES), 0)
    joint = jnp.where(row < part_rows, lane * part_rows + row, joints)
    dims = jnp.zeros((SUBLANES, LANES), jnp.int32)
    for j in range(joints):
        dims = jnp.where(joint == j, hyper_ref[j], dims)
    own = own_ref[...]
    partner = own
    for bit, ref in enumerate(lower_refs):
        partner = jnp.where(dims == bit, ref[...], partner)
    for bit in range(upper_bits):
        other = stepped_of(got_ref, upper ^ (1 << bit))
        partner = jnp.where(dims == len(lower_refs) + bit, other, partner)
    mixed = 0.5 * (own + partner)
    for j in range(per_row):
        turn = (-j * shard) % LANES
        part = pltpu.roll(mixed, turn, 1) if turn else mixed
        for r in range(part_rows):
            out_ref[j * part_rows + r] = part[r : r + 1, :shard]


def local(queries, key_rows, value_rows, cotangent, readout, rand_blocks, global_blocks, hyper_dim):
    heads = lax.axis_size("head")
    uppers = lax.axis_size("upper")
    lowers = lax.axis_size("lower")
    joints = cotangent.shape[1]
    shard = readout.shape[2]
    listed = 3 + rand_blocks.shape[1] + global_blocks.shape[0]
    cot_rows = -(-joints // 32) * 32
    vmem = pl.BlockSpec(memory_space=pltpu.VMEM)
    smem = pl.BlockSpec(memory_space=pltpu.SMEM)
    away_spec = pl.BlockSpec(memory_space=pltpu.HBM)
    params = pltpu.CompilerParams(vmem_limit_bytes=VMEM_LIMIT)
    by_head = (heads, BLOCK, HEAD_SIZE)

    def near(value):
        return pltpu.with_memory_space_constraint(value, pltpu.VMEM)

    def away(value):
        return pltpu.with_memory_space_constraint(value, pltpu.HBM)

    def spread(value):
        return lax.all_to_all(value, "head", split_axis=0, concat_axis=0, tiled=True)

    def swap(value, distance):
        return lax.ppermute(value, "member", [(i, i ^ distance) for i in range(MEMBERS)])

    def split(rows):
        return pl.pallas_call(
            split_heads,
            out_shape=jax.ShapeDtypeStruct(by_head, rows.dtype),
            in_specs=[vmem],
            out_specs=vmem,
            compiler_params=params,
        )(rows)

    split_k = split(key_rows[0])
    k0 = spread(split_k)
    split_v = split(value_rows[0])
    v0 = spread(split_v)
    packed = pl.pallas_call(
        split_queries,
        out_shape=jax.ShapeDtypeStruct((heads, BLOCK + cot_rows, HEAD_SIZE), queries.dtype),
        in_specs=[vmem, vmem],
        out_specs=vmem,
        compiler_params=params,
        name="split_queries",
    )(queries[0], cotangent[0])
    q0 = spread(packed)
    k2 = swap(k0, 2)
    k1 = swap(k0, 1)
    k3 = swap(k2, 1)
    v2 = swap(v0, 2)
    v1 = swap(v0, 1)
    v3 = swap(v2, 1)
    mixed, sent = pl.pallas_call(
        functools.partial(attend, joints),
        out_shape=(
            jax.ShapeDtypeStruct(by_head, jnp.bfloat16),
            jax.ShapeDtypeStruct((uppers * MEMBERS, SUBLANES, LANES), jnp.float32),
        ),
        in_specs=[smem, smem, vmem] + [away_spec] * 3 + [vmem, away_spec] + [vmem] * 4,
        out_specs=(vmem, vmem),
        scratch_shapes=[
            pltpu.VMEM((MEMBERS, *by_head), jnp.bfloat16),
            pltpu.VMEM((MEMBERS, *by_head), jnp.bfloat16),
            pltpu.VMEM((cot_rows, HEAD_SIZE), jnp.float32),
            pltpu.VMEM((cot_rows, LANES), jnp.float32),
            pltpu.VMEM((BLOCK, listed * BLOCK), jnp.float32),
            pltpu.VMEM((BLOCK, listed * BLOCK), jnp.float32),
            pltpu.VMEM((BLOCK, listed * BLOCK), jnp.bfloat16),
            pltpu.VMEM((BLOCK, listed * BLOCK), jnp.bfloat16),
            pltpu.SemaphoreType.DMA((MEMBERS,)),
        ],
        compiler_params=params,
        name="attend",
    )(
        rand_blocks.T,
        global_blocks,
        near(q0),
        away(k0), away(k1), away(k2), near(k3),
        away(v0), near(v1), near(v2), near(v3),
        readout.reshape(joints, 1, shard),
    )
    got = lax.all_to_all(
        sent, ("upper", "member"), split_axis=0, concat_axis=0, tiled=True
    )
    returned = spread(mixed)
    piece = jax.ShapeDtypeStruct((SUBLANES, LANES), jnp.float32)
    stepped = pl.pallas_call(
        own_step,
        out_shape=piece,
        in_specs=[vmem],
        out_specs=vmem,
        compiler_params=params,
        name="own_step",
    )(near(got))
    partners = []
    for bit in range(lowers.bit_length() - 1):
        partners.append(lax.ppermute(stepped, "lower", [(i, i ^ 1 << bit) for i in range(lowers)]))
    attention = pl.pallas_call(
        join_heads,
        out_shape=jax.ShapeDtypeStruct((BLOCK, heads * HEAD_SIZE), returned.dtype),
        in_specs=[vmem],
        out_specs=vmem,
        compiler_params=params,
        name="join_heads",
    )(near(returned))
    new_readout = pl.pallas_call(
        functools.partial(blend, joints),
        out_shape=jax.ShapeDtypeStruct((joints, 1, shard), jnp.float32),
        in_specs=[smem] + [vmem] * (2 + len(partners)),
        out_specs=vmem,
        compiler_params=params,
        name="blend",
    )(hyper_dim, near(got), near(stepped), *map(near, partners))
    return (attention[None], new_readout.reshape(1, joints, shard))


def solution(mesh):
    replicas, group = mesh.devices.shape
    lowers = 1 << (replicas.bit_length() - 1) // 2
    fine = Mesh(
        mesh.devices.reshape(replicas // lowers, lowers, group // MEMBERS, MEMBERS),
        ("upper", "lower", "head", "member"),
    )
    rows = P(("upper", "lower"), ("head", "member"), None)
    columns = P(("upper", "lower"), None, ("head", "member"))
    return jax.shard_map(
        local,
        mesh=fine,
        in_specs=(rows, rows, rows, columns, columns, P(), P(), P()),
        out_specs=(rows, columns),
        check_vma=False,
    )
```

time: 168 us -> 153 us (0.911)
  starting transfers between devices: 94.6 us -> 78.9 us
  blocking collectives: 0 us -> 12.1 us
  Pallas kernels: 22.9 us -> 10.8 us
    all_to_all x0 -> x1, blocking collectives: none -> 12.1 us  [local(): lax.all_to_all(sent, ('upper', 'member'), split_axis=0, concat_axis=0, ti...]
    ppermute x4 -> x2, starting transfers between devices: 34.1 us -> 24.1 us  [local(): lax.ppermute(stepped, 'lower', [(i, i ^ 1 << bit) for i in range(lowers)])]
    ppermute x9 -> x6, starting transfers between devices: 22.2 us -> 14.3 us  [swap(): lax.ppermute(value, 'member', [(i, i ^ distance) for i in range(MEMBERS)])]
    pallas_call x1, Pallas kernels: 13.5 us -> 5.91 us  [local(): pl.pallas_call(functools.partial(attend, joints), out_shape=(jax.ShapeDty...]
    all_to_all x4, starting transfers between devices: 38.3 us -> 40.5 us  [spread(): lax.all_to_all(value, 'head', split_axis=0, concat_axis=0, tiled=True)]
    pallas_call x2, Pallas kernels: 3.89 us -> 1.78 us  [split(): pl.pallas_call(split_heads, out_shape=jax.ShapeDtypeStruct(by_head, rows....]
    all_to_all x4, waiting for transfers between devices: 24.1 us -> 26 us  [spread(): lax.all_to_all(value, 'head', split_axis=0, concat_axis=0, tiled=True)]
    ppermute x9 -> x6, waiting for transfers between devices: 19.9 us -> 18.9 us  [swap(): lax.ppermute(value, 'member', [(i, i ^ distance) for i in range(MEMBERS)])]
  transfers between devices with their start and end apart: 17 -> 12, of which waited for: 8 -> 6; matrix products, arithmetic and copies ran while one was open for 0% -> 0% of each run, Pallas kernels for 3% -> 2%
where the time goes in v2:
time: 153 us; the launch traced here: 152 us
  starting transfers between devices  78.9 us (52%)
  waiting for transfers between devices  47.2 us (31%)
  blocking collectives  12.1 us (8%)
  Pallas kernels  10.8 us (7%)
  local copies, waits for them, and re-layouts  1.73 us (1%)
    all_to_all x4, starting transfers between devices, spread(): lax.all_to_all(value, 'head', split_axis=0, concat_axis=0, tiled=True)  40.5 us
    all_to_all x4, waiting for transfers between devices, spread(): lax.all_to_all(value, 'head', split_axis=0, concat_axis=0, tiled=True)  26 us
    ppermute x2, starting transfers between devices, local(): lax.ppermute(stepped, 'lower', [(i, i ^ 1 << bit) for i in range(lowers)])  24.1 us
    ppermute x6, waiting for transfers between devices, swap(): lax.ppermute(value, 'member', [(i, i ^ distance) for i in range(MEMBERS)])  18.9 us
    ppermute x6, starting transfers between devices, swap(): lax.ppermute(value, 'member', [(i, i ^ distance) for i in range(MEMBERS)])  14.3 us
    all_to_all x1, blocking collectives, local(): lax.all_to_all(sent, ('upper', 'member'), split_axis=0, concat_axis=0, ti...  12.1 us
    pallas_call x1, Pallas kernels, local(): pl.pallas_call(functools.partial(attend, joints), out_shape=(jax.ShapeDty...  5.91 us
  transfers between devices with their start and end apart: 12, of which 6 were waited for; matrix products, arithmetic and copies ran while one was open for 0% of the time, Pallas kernels for 2%

profile of v2, /device:TPU:8, one launch (start us, length us, event | category | flops | bytes accessed | tf_op | source)
XLA Modules:
  0.0 152.2 jit_solution(9278682687895405723)
XLA Ops:
  0.6 1.0 copy-done
  2.6 16.6 %all-to-all-start.1 = ((bf16[16,128,128]{2,1,0:T(8,128)(2,1)}), bf16[16,128,128]{2,1,0:T(8,128)(2,1)S(1)}, u32[]{:S(2)}, u32[]{:S(2)}) async-start(bf16[16,128,128]{2,1,0:T(8,128)(2,1)} %shard_map.95), calls=%async_computation.1 | async-start | bytes 1048576 | tf_op jit(solution)/shard_map/all_to_all | solution.py:224
  20.0 11.2 %all-to-all-done.1.k0 = bf16[16,128,128]{2,1,0:T(8,128)(2,1)S(1)} async-done(((bf16[16,128,128]{2,1,0:T(8,128)(2,1)}), bf16[16,128,128]{2,1,0:T(8,128)(2,1)S(1)}, u32[]{:S(2)}, u32[]{:S(2)}) %all-to-all-start.1) | async-done | bytes 524320 | tf_op jit(solution)/shard_map/all_to_all | solution.py:224
  31.2 5.4 %all-to-all-start.2 = ((bf16[16,128,128]{2,1,0:T(8,128)(2,1)}), bf16[16,128,128]{2,1,0:T(8,128)(2,1)}, u32[]{:S(2)}, u32[]{:S(2)}) async-start(bf16[16,128,128]{2,1,0:T(8,128)(2,1)} %shard_map.96), calls=%async_computation.2 | async-start | bytes 1048576 | tf_op jit(solution)/shard_map/all_to_all | solution.py:224
  36.6 1.0 split_queries.1
  37.6 14.8 %all-to-all-done.2.v0 = bf16[16,128,128]{2,1,0:T(8,128)(2,1)} async-done(((bf16[16,128,128]{2,1,0:T(8,128)(2,1)}), bf16[16,128,128]{2,1,0:T(8,128)(2,1)}, u32[]{:S(2)}, u32[]{:S(2)}) %all-to-all-start.2) | async-done | bytes 524320 | tf_op jit(solution)/shard_map/all_to_all | solution.py:224
  52.4 5.0 %all-to-all-start = ((bf16[16,160,128]{2,1,0:T(8,128)(2,1)}), bf16[16,160,128]{2,1,0:T(8,128)(2,1)S(1)}, u32[]{:S(2)}, u32[]{:S(2)}) async-start(bf16[16,160,128]{2,1,0:T(8,128)(2,1)} %split_queries.1), calls=%async_computation | async-start | bytes 1310720 | tf_op jit(solution)/shard_map/all_to_all | solution.py:224
  57.4 4.2 %collective-permute-start.1 = (bf16[16,128,128]{2,1,0:T(8,128)(2,1)S(1)}, bf16[16,128,128]{2,1,0:T(8,128)(2,1)}, u32[]{:S(2)}, u32[]{:S(2)}) collective-permute-start(bf16[16,128,128]{2,1,0:T(8,128)(2,1)S(1)} %all-to-all-done.1.k0), channel_id=1, source_target_pairs={{0,2},{1,3},{2,0},{3,1},{4,6},{5,7},{6,4},{7,5},{8,10},{9,11},{10,... | collective-permute-start | bytes 1572872 | tf_op jit(solution)/shard_map/ppermute | solution.py:227
  61.6 1.9 %collective-permute-start.4 = (bf16[16,128,128]{2,1,0:T(8,128)(2,1)}, bf16[16,128,128]{2,1,0:T(8,128)(2,1)S(1)}, u32[]{:S(2)}, u32[]{:S(2)}) collective-permute-start(bf16[16,128,128]{2,1,0:T(8,128)(2,1)} %all-to-all-done.2.v0), channel_id=1, source_target_pairs={{0,2},{1,3},{2,0},{3,1},{4,6},{5,7},{6,4},{7,5},{8,10},{9,11},{10,... | collective-permute-start | bytes 1572872 | tf_op jit(solution)/shard_map/ppermute | solution.py:227
  63.5 1.9 %collective-permute-start = (bf16[16,128,128]{2,1,0:T(8,128)(2,1)S(1)}, bf16[16,128,128]{2,1,0:T(8,128)(2,1)}, u32[]{:S(2)}, u32[]{:S(2)}) collective-permute-start(bf16[16,128,128]{2,1,0:T(8,128)(2,1)S(1)} %all-to-all-done.1.k0), channel_id=1, source_target_pairs={{0,1},{1,0},{2,3},{3,2},{4,5},{5,4},{6,7},{7,6},{8,9},{9,8},{10,11... | collective-permute-start | bytes 1572872 | tf_op jit(solution)/shard_map/ppermute | solution.py:227
  65.5 2.4 %collective-permute-start.3 = (bf16[16,128,128]{2,1,0:T(8,128)(2,1)}, bf16[16,128,128]{2,1,0:T(8,128)(2,1)S(1)}, u32[]{:S(2)}, u32[]{:S(2)}) collective-permute-start(bf16[16,128,128]{2,1,0:T(8,128)(2,1)} %all-to-all-done.2.v0), channel_id=1, source_target_pairs={{0,1},{1,0},{2,3},{3,2},{4,5},{5,4},{6,7},{7,6},{8,9},{9,8},{10,11... | collective-permute-start | bytes 1572872 | tf_op jit(solution)/shard_map/ppermute | solution.py:227
  67.9 9.5 %collective-permute-done.1.k2 = bf16[16,128,128]{2,1,0:T(8,128)(2,1)} collective-permute-done((bf16[16,128,128]{2,1,0:T(8,128)(2,1)S(1)}, bf16[16,128,128]{2,1,0:T(8,128)(2,1)}, u32[]{:S(2)}, u32[]{:S(2)}) %collective-permute-start.1) | collective-permute-done | bytes 524320 | tf_op jit(solution)/shard_map/ppermute | solution.py:227
  77.3 1.9 %collective-permute-start.2 = (bf16[16,128,128]{2,1,0:T(8,128)(2,1)}, bf16[16,128,128]{2,1,0:T(8,128)(2,1)S(1)}, u32[]{:S(2)}, u32[]{:S(2)}) collective-permute-start(bf16[16,128,128]{2,1,0:T(8,128)(2,1)} %collective-permute-done.1.k2), channel_id=1, source_target_pairs={{0,1},{1,0},{2,3},{3,2},{4,5},{5,4},{6,7},{7,6},{8,9},{9,8},{10,11... | collective-permute-start | bytes 1572872 | tf_op jit(solution)/shard_map/ppermute | solution.py:227
  79.3 8.2 %collective-permute-done.4.v2 = bf16[16,128,128]{2,1,0:T(8,128)(2,1)S(1)} collective-permute-done((bf16[16,128,128]{2,1,0:T(8,128)(2,1)}, bf16[16,128,128]{2,1,0:T(8,128)(2,1)S(1)}, u32[]{:S(2)}, u32[]{:S(2)}) %collective-permute-start.4) | collective-permute-done | bytes 524320 | tf_op jit(solution)/shard_map/ppermute | solution.py:227
  87.5 1.9 %collective-permute-start.5 = (bf16[16,128,128]{2,1,0:T(8,128)(2,1)S(1)}, bf16[16,128,128]{2,1,0:T(8,128)(2,1)S(1)}, u32[]{:S(2)}, u32[]{:S(2)}) collective-permute-start(bf16[16,128,128]{2,1,0:T(8,128)(2,1)S(1)} %collective-permute-done.4.v2), channel_id=1, source_target_pairs={{0,1},{1,0},{2,3},{3,2},{4,5},{5,4},{6,7},{7,6},{8,9},{9,8},{10,11... | collective-permute-start | bytes 1572872 | tf_op jit(solution)/shard_map/ppermute | solution.py:227
  90.1 1.2 collective-permute-done.5.v3
  91.9 5.9 %attend.1 = (bf16[16,128,128]{2,1,0:T(8,128)(2,1)}, f32[16,8,128]{2,1,0:T(8,128)S(1)}) custom-call(s32[2,64]{1,0:T(2,128)S(1)} %bitcast.13, s32[1]{0:T(128)S(6)} %copy.10.global_ref, bf16[16,160,128]{2,1,0:T(8,128)(2,1)S(1)} %all-to-all-done.query_ref, bf16[16,128,128]{2,1,0:T(8,128)(2,1)} %copy-done.7, bf16[16,128,128]{2,1,0:T(8,128)(2,1)} %collective-permute-done.k1, ...), custom_call_target="tpu_custom_call" | custom-call | tf_op jit(solution)/shard_map/attend/pallas_call | solution.py:257
  97.8 12.1 %all_to_all.25.got_ref = f32[16,8,128]{2,1,0:T(8,128)S(1)} all-to-all(f32[16,8,128]{2,1,0:T(8,128)S(1)} %get-tuple-element.5), channel_id=1, replica_groups=mesh['upper'=4,'lower'=4,'head'=16,'member'=4] {'upper','member'}, dimensions={0} | all-to-all | bytes 131072 | tf_op jit(solution)/shard_map/all_to_all | solution.py:286
  110.0 13.6 %all-to-all-start.3 = ((bf16[16,128,128]{2,1,0:T(8,128)(2,1)}), bf16[16,128,128]{2,1,0:T(8,128)(2,1)S(1)}, u32[]{:S(2)}, u32[]{:S(2)}) async-start(bf16[16,128,128]{2,1,0:T(8,128)(2,1)} %get-tuple-element.4), calls=%async_computation.3 | async-start | bytes 1048576 | tf_op jit(solution)/shard_map/all_to_all | solution.py:224
  123.6 10.9 %collective-permute-start.6 = (f32[8,128]{1,0:T(8,128)S(1)}, f32[8,128]{1,0:T(8,128)S(1)}, u32[]{:S(2)}, u32[]{:S(2)}) collective-permute-start(f32[8,128]{1,0:T(8,128)S(1)} %own_step.1.own_ref), channel_id=1, source_target_pairs={{0,64},{64,0},{128,192},{192,128},{1,65},{65,1},{129,193},{193,129... | collective-permute-start | bytes 12296 | tf_op jit(solution)/shard_map/ppermute | solution.py:301
  134.6 13.2 %collective-permute-start.7 = (f32[8,128]{1,0:T(8,128)S(1)}, f32[8,128]{1,0:T(8,128)S(1)}, u32[]{:S(2)}, u32[]{:S(2)}) collective-permute-start(f32[8,128]{1,0:T(8,128)S(1)} %own_step.1.own_ref), channel_id=1, source_target_pairs={{0,128},{64,192},{128,0},{192,64},{1,129},{65,193},{129,1},{193,65... | collective-permute-start | bytes 12296 | tf_op jit(solution)/shard_map/ppermute | solution.py:301
  147.7 2.3 %collective-permute-done.7.refs_1_ = f32[8,128]{1,0:T(8,128)S(1)} collective-permute-done((f32[8,128]{1,0:T(8,128)S(1)}, f32[8,128]{1,0:T(8,128)S(1)}, u32[]{:S(2)}, u32[]{:S(2)}) %collective-permute-start.7) | collective-permute-done | bytes 4128 | tf_op jit(solution)/shard_map/ppermute | solution.py:301
  150.0 1.2 blend.1
  151.3 0.9 join_heads.1
  (24 shorter events, 2.5 us)
Async XLA Ops:
  0.6 1.0 copy-start
  2.6 16.6 %copy-start.1 = (bf16[1,128,2048]{2,1,0:T(8,128)(2,1)S(1)}, bf16[1,128,2048]{2,1,0:T(8,128)(2,1)}, u32[]{:S(2)}) copy-start(bf16[1,128,2048]{2,1,0:T(8,128)(2,1)} %param.10) | copy-start | bytes 1572868
  2.6 28.6 %all-to-all-start.1 = ((bf16[16,128,128]{2,1,0:T(8,128)(2,1)}), bf16[16,128,128]{2,1,0:T(8,128)(2,1)S(1)}, u32[]{:S(2)}, u32[]{:S(2)}) async-start(bf16[16,128,128]{2,1,0:T(8,128)(2,1)} %shard_map.95), calls=%async_computation.1 | async-start | bytes 1048576 | tf_op jit(solution)/shard_map/all_to_all | solution.py:224
  20.0 16.6 %copy-start.2 = (bf16[1,128,2048]{2,1,0:T(8,128)(2,1)S(1)}, bf16[1,128,2048]{2,1,0:T(8,128)(2,1)}, u32[]{:S(2)}) copy-start(bf16[1,128,2048]{2,1,0:T(8,128)(2,1)} %param.8) | copy-start | bytes 1572868
  31.2 32.3 %copy-start.7 = (bf16[16,128,128]{2,1,0:T(8,128)(2,1)}, bf16[16,128,128]{2,1,0:T(8,128)(2,1)S(1)}, u32[]{:S(2)}) copy-start(bf16[16,128,128]{2,1,0:T(8,128)(2,1)S(1)} %all-to-all-done.1.k0) | copy-start | bytes 1572868
  31.2 5.4 %copy-start.4 = (bf16[1,20,128]{2,1,0:T(8,128)(2,1)S(1)}, bf16[1,20,128]{2,1,0:T(8,128)(2,1)}, u32[]{:S(2)}) copy-start(bf16[1,20,128]{2,1,0:T(8,128)(2,1)} %param.11) | copy-start | bytes 15364
  31.2 21.2 %all-to-all-start.2 = ((bf16[16,128,128]{2,1,0:T(8,128)(2,1)}), bf16[16,128,128]{2,1,0:T(8,128)(2,1)}, u32[]{:S(2)}, u32[]{:S(2)}) async-start(bf16[16,128,128]{2,1,0:T(8,128)(2,1)} %shard_map.96), calls=%async_computation.2 | async-start | bytes 1048576 | tf_op jit(solution)/shard_map/all_to_all | solution.py:224
  52.4 38.8 %copy-start.3 = (f32[1,20,32]{2,0,1:T(1,128)S(1)}, f32[1,20,32]{2,0,1:T(1,128)}, u32[]{:S(2)}) copy-start(f32[1,20,32]{2,0,1:T(1,128)} %param.12) | copy-start | bytes 7684
  52.4 37.6 %all-to-all-start = ((bf16[16,160,128]{2,1,0:T(8,128)(2,1)}), bf16[16,160,128]{2,1,0:T(8,128)(2,1)S(1)}, u32[]{:S(2)}, u32[]{:S(2)}) async-start(bf16[16,160,128]{2,1,0:T(8,128)(2,1)} %split_queries.1), calls=%async_computation | async-start | bytes 1310720 | tf_op jit(solution)/shard_map/all_to_all | solution.py:224
  57.4 20.0 %collective-permute-start.1 = (bf16[16,128,128]{2,1,0:T(8,128)(2,1)S(1)}, bf16[16,128,128]{2,1,0:T(8,128)(2,1)}, u32[]{:S(2)}, u32[]{:S(2)}) collective-permute-start(bf16[16,128,128]{2,1,0:T(8,128)(2,1)S(1)} %all-to-all-done.1.k0), channel_id=1, source_target_pairs={{0,2},{1,3},{2,0},{3,1},{4,6},{5,7},{6,4},{7,5},{8,10},{9,11},{10,... | collective-permute-start | bytes 1572872 | tf_op jit(solution)/shard_map/ppermute | solution.py:227
  61.6 25.9 %collective-permute-start.4 = (bf16[16,128,128]{2,1,0:T(8,128)(2,1)}, bf16[16,128,128]{2,1,0:T(8,128)(2,1)S(1)}, u32[]{:S(2)}, u32[]{:S(2)}) collective-permute-start(bf16[16,128,128]{2,1,0:T(8,128)(2,1)} %all-to-all-done.2.v0), channel_id=1, source_target_pairs={{0,2},{1,3},{2,0},{3,1},{4,6},{5,7},{6,4},{7,5},{8,10},{9,11},{10,... | collective-permute-start | bytes 1572872 | tf_op jit(solution)/shard_map/ppermute | solution.py:227
  63.5 26.5 %collective-permute-start = (bf16[16,128,128]{2,1,0:T(8,128)(2,1)S(1)}, bf16[16,128,128]{2,1,0:T(8,128)(2,1)}, u32[]{:S(2)}, u32[]{:S(2)}) collective-permute-start(bf16[16,128,128]{2,1,0:T(8,128)(2,1)S(1)} %all-to-all-done.1.k0), channel_id=1, source_target_pairs={{0,1},{1,0},{2,3},{3,2},{4,5},{5,4},{6,7},{7,6},{8,9},{9,8},{10,11... | collective-permute-start | bytes 1572872 | tf_op jit(solution)/shard_map/ppermute | solution.py:227
  65.5 24.6 %collective-permute-start.3 = (bf16[16,128,128]{2,1,0:T(8,128)(2,1)}, bf16[16,128,128]{2,1,0:T(8,128)(2,1)S(1)}, u32[]{:S(2)}, u32[]{:S(2)}) collective-permute-start(bf16[16,128,128]{2,1,0:T(8,128)(2,1)} %all-to-all-done.2.v0), channel_id=1, source_target_pairs={{0,1},{1,0},{2,3},{3,2},{4,5},{5,4},{6,7},{7,6},{8,9},{9,8},{10,11... | collective-permute-start | bytes 1572872 | tf_op jit(solution)/shard_map/ppermute | solution.py:227
  77.3 12.7 %collective-permute-start.2 = (bf16[16,128,128]{2,1,0:T(8,128)(2,1)}, bf16[16,128,128]{2,1,0:T(8,128)(2,1)S(1)}, u32[]{:S(2)}, u32[]{:S(2)}) collective-permute-start(bf16[16,128,128]{2,1,0:T(8,128)(2,1)} %collective-permute-done.1.k2), channel_id=1, source_target_pairs={{0,1},{1,0},{2,3},{3,2},{4,5},{5,4},{6,7},{7,6},{8,9},{9,8},{10,11... | collective-permute-start | bytes 1572872 | tf_op jit(solution)/shard_map/ppermute | solution.py:227
  87.5 3.8 %collective-permute-start.5 = (bf16[16,128,128]{2,1,0:T(8,128)(2,1)S(1)}, bf16[16,128,128]{2,1,0:T(8,128)(2,1)S(1)}, u32[]{:S(2)}, u32[]{:S(2)}) collective-permute-start(bf16[16,128,128]{2,1,0:T(8,128)(2,1)S(1)} %collective-permute-done.4.v2), channel_id=1, source_target_pairs={{0,1},{1,0},{2,3},{3,2},{4,5},{5,4},{6,7},{7,6},{8,9},{9,8},{10,11... | collective-permute-start | bytes 1572872 | tf_op jit(solution)/shard_map/ppermute | solution.py:227
  91.2 0.7 copy-start.5
  110.0 41.3 %all-to-all-start.3 = ((bf16[16,128,128]{2,1,0:T(8,128)(2,1)}), bf16[16,128,128]{2,1,0:T(8,128)(2,1)S(1)}, u32[]{:S(2)}, u32[]{:S(2)}) async-start(bf16[16,128,128]{2,1,0:T(8,128)(2,1)} %get-tuple-element.4), calls=%async_computation.3 | async-start | bytes 1048576 | tf_op jit(solution)/shard_map/all_to_all | solution.py:224
  123.6 26.4 %copy-start.6 = (s32[20]{0:T(128)S(1)}, s32[20]{0:T(128)}, u32[]{:S(2)}) copy-start(s32[20]{0:T(128)} %hyper_ref.1) | copy-start | bytes 244
  123.6 24.1 %collective-permute-start.6 = (f32[8,128]{1,0:T(8,128)S(1)}, f32[8,128]{1,0:T(8,128)S(1)}, u32[]{:S(2)}, u32[]{:S(2)}) collective-permute-start(f32[8,128]{1,0:T(8,128)S(1)} %own_step.1.own_ref), channel_id=1, source_target_pairs={{0,64},{64,0},{128,192},{192,128},{1,65},{65,1},{129,193},{193,129... | collective-permute-start | bytes 12296 | tf_op jit(solution)/shard_map/ppermute | solution.py:301
  134.6 15.5 %collective-permute-start.7 = (f32[8,128]{1,0:T(8,128)S(1)}, f32[8,128]{1,0:T(8,128)S(1)}, u32[]{:S(2)}, u32[]{:S(2)}) collective-permute-start(f32[8,128]{1,0:T(8,128)S(1)} %own_step.1.own_ref), channel_id=1, source_target_pairs={{0,128},{64,192},{128,0},{192,64},{1,129},{65,193},{129,1},{193,65... | collective-permute-start | bytes 12296 | tf_op jit(solution)/shard_map/ppermute | solution.py:301

commit v3 on v2

--- a/solution.py
+++ b/solution.py
@@ -43,8 +43,7 @@
 
 def attend(
     joints,
-    rand_ref,
-    global_ref,
+    listing_ref,
     query_ref,
     k0, k1, k2, k3,
     v0, v1, v2, v3,
@@ -84,8 +83,7 @@
     def listed(at):
         block = at * MEMBERS + member
         ids = [block, jnp.maximum(block - 1, 0), jnp.minimum(block + 1, blocks - 1)]
-        ids += [rand_ref[c, block] for c in range(rand_ref.shape[0])]
-        ids += [global_ref[c] for c in range(global_ref.shape[0])]
+        ids += [listing_ref[c, block] for c in range(listing_ref.shape[0])]
         return block, [((b & (MEMBERS - 1)) ^ member, b >> MEMBER_BITS) for b in ids]
 
     def score(at, into):
@@ -187,11 +185,17 @@
         dims = jnp.where(joint == j, hyper_ref[j], dims)
     own = own_ref[...]
     partner = own
-    for bit, ref in enumerate(lower_refs):
-        partner = jnp.where(dims == bit, ref[...], partner)
+    lower = lax.axis_index("lower")
+    lower_bits = len(lower_refs) // 2
+    for bit in range(lower_bits):
+        below, above = lower_refs[bit][...], lower_refs[lower_bits + bit][...]
+        if bit == 0:
+            above = jnp.where(lower == 1, above, lower_refs[-1][...])
+        got = jnp.where((lower >> bit) & 1 == 0, below, above)
+        partner = jnp.where(dims == bit, got, partner)
     for bit in range(upper_bits):
         other = stepped_of(got_ref, upper ^ (1 << bit))
-        partner = jnp.where(dims == len(lower_refs) + bit, other, partner)
+        partner = jnp.where(dims == lower_bits + bit, other, partner)
     mixed = 0.5 * (own + partner)
     for j in range(per_row):
         turn = (-j * shard) % LANES
@@ -207,7 +211,7 @@
     joints = cotangent.shape[1]
     shard = readout.shape[2]
     listed = 3 + rand_blocks.shape[1] + global_blocks.shape[0]
-    cot_rows = -(-joints // 32) * 32
+    cot_rows = -(-joints // SUBLANES) * SUBLANES
     vmem = pl.BlockSpec(memory_space=pltpu.VMEM)
     smem = pl.BlockSpec(memory_space=pltpu.SMEM)
     away_spec = pl.BlockSpec(memory_space=pltpu.HBM)
@@ -235,6 +239,9 @@
             compiler_params=params,
         )(rows)
 
+    listing = jnp.concatenate(
+        [rand_blocks.T, jnp.broadcast_to(global_blocks[:, None], (global_blocks.shape[0], rand_blocks.shape[0]))]
+    )
     split_k = split(key_rows[0])
     k0 = spread(split_k)
     split_v = split(value_rows[0])
@@ -260,7 +267,7 @@
             jax.ShapeDtypeStruct(by_head, jnp.bfloat16),
             jax.ShapeDtypeStruct((uppers * MEMBERS, SUBLANES, LANES), jnp.float32),
         ),
-        in_specs=[smem, smem, vmem] + [away_spec] * 3 + [vmem, away_spec] + [vmem] * 4,
+        in_specs=[smem, vmem] + [away_spec] * 3 + [vmem, away_spec] + [vmem] * 4,
         out_specs=(vmem, vmem),
         scratch_shapes=[
             pltpu.VMEM((MEMBERS, *by_head), jnp.bfloat16),
@@ -276,8 +283,7 @@
         compiler_params=params,
         name="attend",
     )(
-        rand_blocks.T,
-        global_blocks,
+        listing,
         near(q0),
         away(k0), away(k1), away(k2), near(k3),
         away(v0), near(v1), near(v2), near(v3),
@@ -296,9 +302,19 @@
         compiler_params=params,
         name="own_step",
     )(near(got))
-    partners = []
-    for bit in range(lowers.bit_length() - 1):
-        partners.append(lax.ppermute(stepped, "lower", [(i, i ^ 1 << bit) for i in range(lowers)]))
+
+    def passed(bit, senders):
+        pairs = [(i, i ^ 1 << bit) for i in senders]
+        return lax.ppermute(stepped, "lower", pairs) if pairs else stepped
+
+    bits = range(lowers.bit_length() - 1)
+    ones = [[i for i in range(lowers) if i >> bit & 1] for bit in bits]
+    zeros = [[i for i in range(lowers) if not i >> bit & 1] for bit in bits]
+    partners = [passed(bit, ones[bit]) for bit in bits]
+    if partners:
+        partners.append(passed(0, zeros[0][:1]))
+        partners += [passed(bit, zeros[bit]) for bit in bits[1:]]
+        partners.append(passed(0, zeros[0][1:]))
     attention = pl.pallas_call(
         join_heads,
         out_shape=jax.ShapeDtypeStruct((BLOCK, heads * HEAD_SIZE), returned.dtype),

time: 153 us -> 150 us (0.980)
  starting transfers between devices: 78.9 us -> 76.8 us
    ppermute x2 -> x5, starting transfers between devices: 24.1 us -> 22 us  [passed(): return lax.ppermute(stepped, 'lower', pairs) if pairs else stepped]
  transfers between devices with their start and end apart: 12 -> 15, of which waited for: 6 -> 6; matrix products, arithmetic and copies ran while one was open for 0% -> 0% of each run, Pallas kernels for 2% -> 2%
where the time goes in v3:
time: 150 us; the launch traced here: 149 us
  starting transfers between devices  76.8 us (51%)
  waiting for transfers between devices  46.9 us (31%)
  blocking collectives  12 us (8%)
  Pallas kernels  10.8 us (7%)
  between operations  1.5 us (1%)
    all_to_all x4, starting transfers between devices, spread(): lax.all_to_all(value, 'head', split_axis=0, concat_axis=0, tiled=True)  40.5 us
    all_to_all x4, waiting for transfers between devices, spread(): lax.all_to_all(value, 'head', split_axis=0, concat_axis=0, tiled=True)  26 us
    ppermute x5, starting transfers between devices, passed(): return lax.ppermute(stepped, 'lower', pairs) if pairs else stepped  22 us
    ppermute x6, waiting for transfers between devices, swap(): lax.ppermute(value, 'member', [(i, i ^ distance) for i in range(MEMBERS)])  18.6 us
    ppermute x6, starting transfers between devices, swap(): lax.ppermute(value, 'member', [(i, i ^ distance) for i in range(MEMBERS)])  14.3 us
    all_to_all x1, blocking collectives, local(): lax.all_to_all(sent, ('upper', 'member'), split_axis=0, concat_axis=0, ti...  12 us
    pallas_call x1, Pallas kernels, local(): pl.pallas_call(functools.partial(attend, joints), out_shape=(jax.ShapeDty...  5.92 us
  transfers between devices with their start and end apart: 15, of which 6 were waited for; matrix products, arithmetic and copies ran while one was open for 0% of the time, Pallas kernels for 2%

profile of v3, /device:TPU:8, one launch (start us, length us, event | category | flops | bytes accessed | tf_op | source)
XLA Modules:
  0.0 149.1 jit_solution(3153760087966456387)
XLA Ops:
  0.6 1.0 copy-done
  2.6 16.6 %all-to-all-start.1 = ((bf16[16,128,128]{2,1,0:T(8,128)(2,1)}), bf16[16,128,128]{2,1,0:T(8,128)(2,1)S(1)}, u32[]{:S(2)}, u32[]{:S(2)}) async-start(bf16[16,128,128]{2,1,0:T(8,128)(2,1)} %shard_map.95), calls=%async_computation.1 | async-start | bytes 1048576 | tf_op jit(solution)/shard_map/all_to_all | solution.py:228
  20.0 11.2 %all-to-all-done.1.k0 = bf16[16,128,128]{2,1,0:T(8,128)(2,1)S(1)} async-done(((bf16[16,128,128]{2,1,0:T(8,128)(2,1)}), bf16[16,128,128]{2,1,0:T(8,128)(2,1)S(1)}, u32[]{:S(2)}, u32[]{:S(2)}) %all-to-all-start.1) | async-done | bytes 524320 | tf_op jit(solution)/shard_map/all_to_all | solution.py:228
  31.2 5.4 %all-to-all-start.2 = ((bf16[16,128,128]{2,1,0:T(8,128)(2,1)}), bf16[16,128,128]{2,1,0:T(8,128)(2,1)}, u32[]{:S(2)}, u32[]{:S(2)}) async-start(bf16[16,128,128]{2,1,0:T(8,128)(2,1)} %shard_map.96), calls=%async_computation.2 | async-start | bytes 1048576 | tf_op jit(solution)/shard_map/all_to_all | solution.py:228
  37.5 14.9 %all-to-all-done.2.v0 = bf16[16,128,128]{2,1,0:T(8,128)(2,1)} async-done(((bf16[16,128,128]{2,1,0:T(8,128)(2,1)}), bf16[16,128,128]{2,1,0:T(8,128)(2,1)}, u32[]{:S(2)}, u32[]{:S(2)}) %all-to-all-start.2) | async-done | bytes 524320 | tf_op jit(solution)/shard_map/all_to_all | solution.py:228
  52.4 5.0 %all-to-all-start = ((bf16[16,152,128]{2,1,0:T(8,128)(2,1)}), bf16[16,152,128]{2,1,0:T(8,128)(2,1)S(1)}, u32[]{:S(2)}, u32[]{:S(2)}) async-start(bf16[16,152,128]{2,1,0:T(8,128)(2,1)} %split_queries.1), calls=%async_computation | async-start | bytes 1245184 | tf_op jit(solution)/shard_map/all_to_all | solution.py:228
  57.4 4.2 %collective-permute-start.1 = (bf16[16,128,128]{2,1,0:T(8,128)(2,1)S(1)}, bf16[16,128,128]{2,1,0:T(8,128)(2,1)}, u32[]{:S(2)}, u32[]{:S(2)}) collective-permute-start(bf16[16,128,128]{2,1,0:T(8,128)(2,1)S(1)} %all-to-all-done.1.k0), channel_id=1, source_target_pairs={{0,2},{1,3},{2,0},{3,1},{4,6},{5,7},{6,4},{7,5},{8,10},{9,11},{10,... | collective-permute-start | bytes 1572872 | tf_op jit(solution)/shard_map/ppermute | solution.py:231
  61.6 1.9 %collective-permute-start.4 = (bf16[16,128,128]{2,1,0:T(8,128)(2,1)}, bf16[16,128,128]{2,1,0:T(8,128)(2,1)S(1)}, u32[]{:S(2)}, u32[]{:S(2)}) collective-permute-start(bf16[16,128,128]{2,1,0:T(8,128)(2,1)} %all-to-all-done.2.v0), channel_id=1, source_target_pairs={{0,2},{1,3},{2,0},{3,1},{4,6},{5,7},{6,4},{7,5},{8,10},{9,11},{10,... | collective-permute-start | bytes 1572872 | tf_op jit(solution)/shard_map/ppermute | solution.py:231
  63.5 1.9 %collective-permute-start = (bf16[16,128,128]{2,1,0:T(8,128)(2,1)S(1)}, bf16[16,128,128]{2,1,0:T(8,128)(2,1)}, u32[]{:S(2)}, u32[]{:S(2)}) collective-permute-start(bf16[16,128,128]{2,1,0:T(8,128)(2,1)S(1)} %all-to-all-done.1.k0), channel_id=1, source_target_pairs={{0,1},{1,0},{2,3},{3,2},{4,5},{5,4},{6,7},{7,6},{8,9},{9,8},{10,11... | collective-permute-start | bytes 1572872 | tf_op jit(solution)/shard_map/ppermute | solution.py:231
  65.5 2.4 %collective-permute-start.3 = (bf16[16,128,128]{2,1,0:T(8,128)(2,1)}, bf16[16,128,128]{2,1,0:T(8,128)(2,1)S(1)}, u32[]{:S(2)}, u32[]{:S(2)}) collective-permute-start(bf16[16,128,128]{2,1,0:T(8,128)(2,1)} %all-to-all-done.2.v0), channel_id=1, source_target_pairs={{0,1},{1,0},{2,3},{3,2},{4,5},{5,4},{6,7},{7,6},{8,9},{9,8},{10,11... | collective-permute-start | bytes 1572872 | tf_op jit(solution)/shard_map/ppermute | solution.py:231
  67.9 9.3 %collective-permute-done.1.k2 = bf16[16,128,128]{2,1,0:T(8,128)(2,1)} collective-permute-done((bf16[16,128,128]{2,1,0:T(8,128)(2,1)S(1)}, bf16[16,128,128]{2,1,0:T(8,128)(2,1)}, u32[]{:S(2)}, u32[]{:S(2)}) %collective-permute-start.1) | collective-permute-done | bytes 524320 | tf_op jit(solution)/shard_map/ppermute | solution.py:231
  77.2 1.9 %collective-permute-start.2 = (bf16[16,128,128]{2,1,0:T(8,128)(2,1)}, bf16[16,128,128]{2,1,0:T(8,128)(2,1)S(1)}, u32[]{:S(2)}, u32[]{:S(2)}) collective-permute-start(bf16[16,128,128]{2,1,0:T(8,128)(2,1)} %collective-permute-done.1.k2), channel_id=1, source_target_pairs={{0,1},{1,0},{2,3},{3,2},{4,5},{5,4},{6,7},{7,6},{8,9},{9,8},{10,11... | collective-permute-start | bytes 1572872 | tf_op jit(solution)/shard_map/ppermute | solution.py:231
  79.1 8.2 %collective-permute-done.4.v2 = bf16[16,128,128]{2,1,0:T(8,128)(2,1)S(1)} collective-permute-done((bf16[16,128,128]{2,1,0:T(8,128)(2,1)}, bf16[16,128,128]{2,1,0:T(8,128)(2,1)S(1)}, u32[]{:S(2)}, u32[]{:S(2)}) %collective-permute-start.4) | collective-permute-done | bytes 524320 | tf_op jit(solution)/shard_map/ppermute | solution.py:231
  87.3 1.9 %collective-permute-start.5 = (bf16[16,128,128]{2,1,0:T(8,128)(2,1)S(1)}, bf16[16,128,128]{2,1,0:T(8,128)(2,1)S(1)}, u32[]{:S(2)}, u32[]{:S(2)}) collective-permute-start(bf16[16,128,128]{2,1,0:T(8,128)(2,1)S(1)} %collective-permute-done.4.v2), channel_id=1, source_target_pairs={{0,1},{1,0},{2,3},{3,2},{4,5},{5,4},{6,7},{7,6},{8,9},{9,8},{10,11... | collective-permute-start | bytes 1572872 | tf_op jit(solution)/shard_map/ppermute | solution.py:231
  89.9 1.2 collective-permute-done.5.v3
  91.1 5.9 %attend.1 = (bf16[16,128,128]{2,1,0:T(8,128)(2,1)}, f32[16,8,128]{2,1,0:T(8,128)S(1)}) custom-call(s32[3,64]{1,0:T(4,128)S(1)} %concatenate.3.listing_ref, bf16[16,152,128]{2,1,0:T(8,128)(2,1)S(1)} %all-to-all-done.query_ref, bf16[16,128,128]{2,1,0:T(8,128)(2,1)} %copy-done.6, bf16[16,128,128]{2,1,0:T(8,128)(2,1)} %collective-permute-done.k1, ...), custom_call_target="tpu_custom_call" | custom-call | tf_op jit(solution)/shard_map/attend/pallas_call | solution.py:264
  97.0 12.0 %all_to_all.25.got_ref = f32[16,8,128]{2,1,0:T(8,128)S(1)} all-to-all(f32[16,8,128]{2,1,0:T(8,128)S(1)} %get-tuple-element.5), channel_id=1, replica_groups=mesh['upper'=4,'lower'=4,'head'=16,'member'=4] {'upper','member'}, dimensions={0} | all-to-all | bytes 131072 | tf_op jit(solution)/shard_map/all_to_all | solution.py:292
  109.0 13.6 %all-to-all-start.3 = ((bf16[16,128,128]{2,1,0:T(8,128)(2,1)}), bf16[16,128,128]{2,1,0:T(8,128)(2,1)S(1)}, u32[]{:S(2)}, u32[]{:S(2)}) async-start(bf16[16,128,128]{2,1,0:T(8,128)(2,1)} %get-tuple-element.4), calls=%async_computation.3 | async-start | bytes 1048576 | tf_op jit(solution)/shard_map/all_to_all | solution.py:228
  122.6 1.3 collective-permute-start.6
  123.9 1.3 collective-permute-start.7
  125.2 10.9 %collective-permute-start.8 = (f32[8,128]{1,0:T(8,128)S(1)}, f32[8,128]{1,0:T(8,128)S(1)}, u32[]{:S(2)}, u32[]{:S(2)}) collective-permute-start(f32[8,128]{1,0:T(8,128)S(1)} %own_step.1.own_ref), channel_id=1, source_target_pairs={{0,64},{1,65},{2,66},{3,67},{4,68},{5,69},{6,70},{7,71},{8,72},{9,... | collective-permute-start | bytes 12296 | tf_op jit(solution)/shard_map/ppermute | solution.py:308
  136.1 7.8 %collective-permute-start.9 = (f32[8,128]{1,0:T(8,128)S(1)}, f32[8,128]{1,0:T(8,128)S(1)}, u32[]{:S(2)}, u32[]{:S(2)}) collective-permute-start(f32[8,128]{1,0:T(8,128)S(1)} %own_step.1.own_ref), channel_id=1, source_target_pairs={{0,128},{64,192},{1,129},{65,193},{2,130},{66,194},{3,131},{67,195... | collective-permute-start | bytes 12296 | tf_op jit(solution)/shard_map/ppermute | solution.py:308
  144.6 2.3 %collective-permute-done.7.refs_1_ = f32[8,128]{1,0:T(8,128)S(1)} collective-permute-done((f32[8,128]{1,0:T(8,128)S(1)}, f32[8,128]{1,0:T(8,128)S(1)}, u32[]{:S(2)}, u32[]{:S(2)}) %collective-permute-start.7) | collective-permute-done | bytes 4128 | tf_op jit(solution)/shard_map/ppermute | solution.py:308
  146.9 1.2 blend.1
  (31 shorter events, 4.4 us)
Async XLA Ops:
  0.6 1.0 copy-start
  2.6 16.6 %copy-start.1 = (bf16[1,128,2048]{2,1,0:T(8,128)(2,1)S(1)}, bf16[1,128,2048]{2,1,0:T(8,128)(2,1)}, u32[]{:S(2)}) copy-start(bf16[1,128,2048]{2,1,0:T(8,128)(2,1)} %param.10) | copy-start | bytes 1572868
  2.6 28.6 %all-to-all-start.1 = ((bf16[16,128,128]{2,1,0:T(8,128)(2,1)}), bf16[16,128,128]{2,1,0:T(8,128)(2,1)S(1)}, u32[]{:S(2)}, u32[]{:S(2)}) async-start(bf16[16,128,128]{2,1,0:T(8,128)(2,1)} %shard_map.95), calls=%async_computation.1 | async-start | bytes 1048576 | tf_op jit(solution)/shard_map/all_to_all | solution.py:228
  20.0 16.5 %copy-start.2 = (bf16[1,128,2048]{2,1,0:T(8,128)(2,1)S(1)}, bf16[1,128,2048]{2,1,0:T(8,128)(2,1)}, u32[]{:S(2)}) copy-start(bf16[1,128,2048]{2,1,0:T(8,128)(2,1)} %param.8) | copy-start | bytes 1572868
  31.2 32.3 %copy-start.6 = (bf16[16,128,128]{2,1,0:T(8,128)(2,1)}, bf16[16,128,128]{2,1,0:T(8,128)(2,1)S(1)}, u32[]{:S(2)}) copy-start(bf16[16,128,128]{2,1,0:T(8,128)(2,1)S(1)} %all-to-all-done.1.k0) | copy-start | bytes 1572868
  31.2 5.4 %copy-start.4 = (bf16[1,20,128]{2,1,0:T(8,128)(2,1)S(1)}, bf16[1,20,128]{2,1,0:T(8,128)(2,1)}, u32[]{:S(2)}) copy-start(bf16[1,20,128]{2,1,0:T(8,128)(2,1)} %param.11) | copy-start | bytes 15364
  31.2 21.2 %all-to-all-start.2 = ((bf16[16,128,128]{2,1,0:T(8,128)(2,1)}), bf16[16,128,128]{2,1,0:T(8,128)(2,1)}, u32[]{:S(2)}, u32[]{:S(2)}) async-start(bf16[16,128,128]{2,1,0:T(8,128)(2,1)} %shard_map.96), calls=%async_computation.2 | async-start | bytes 1048576 | tf_op jit(solution)/shard_map/all_to_all | solution.py:228
  52.4 37.4 %copy-start.7 = (s32[64,2]{0,1:T(2,128)S(1)}, s32[64,2]{0,1:T(2,128)}, u32[]{:S(2)}) copy-start(s32[64,2]{0,1:T(2,128)} %param.13) | copy-start | bytes 1540
  52.4 37.5 %all-to-all-start = ((bf16[16,152,128]{2,1,0:T(8,128)(2,1)}), bf16[16,152,128]{2,1,0:T(8,128)(2,1)S(1)}, u32[]{:S(2)}, u32[]{:S(2)}) async-start(bf16[16,152,128]{2,1,0:T(8,128)(2,1)} %split_queries.1), calls=%async_computation | async-start | bytes 1245184 | tf_op jit(solution)/shard_map/all_to_all | solution.py:228
  57.4 33.7 %copy-start.3 = (f32[1,20,32]{2,0,1:T(1,128)S(1)}, f32[1,20,32]{2,0,1:T(1,128)}, u32[]{:S(2)}) copy-start(f32[1,20,32]{2,0,1:T(1,128)} %param.12) | copy-start | bytes 7684
  57.4 19.8 %collective-permute-start.1 = (bf16[16,128,128]{2,1,0:T(8,128)(2,1)S(1)}, bf16[16,128,128]{2,1,0:T(8,128)(2,1)}, u32[]{:S(2)}, u32[]{:S(2)}) collective-permute-start(bf16[16,128,128]{2,1,0:T(8,128)(2,1)S(1)} %all-to-all-done.1.k0), channel_id=1, source_target_pairs={{0,2},{1,3},{2,0},{3,1},{4,6},{5,7},{6,4},{7,5},{8,10},{9,11},{10,... | collective-permute-start | bytes 1572872 | tf_op jit(solution)/shard_map/ppermute | solution.py:231
  61.6 25.7 %collective-permute-start.4 = (bf16[16,128,128]{2,1,0:T(8,128)(2,1)}, bf16[16,128,128]{2,1,0:T(8,128)(2,1)S(1)}, u32[]{:S(2)}, u32[]{:S(2)}) collective-permute-start(bf16[16,128,128]{2,1,0:T(8,128)(2,1)} %all-to-all-done.2.v0), channel_id=1, source_target_pairs={{0,2},{1,3},{2,0},{3,1},{4,6},{5,7},{6,4},{7,5},{8,10},{9,11},{10,... | collective-permute-start | bytes 1572872 | tf_op jit(solution)/shard_map/ppermute | solution.py:231
  63.5 26.3 %collective-permute-start = (bf16[16,128,128]{2,1,0:T(8,128)(2,1)S(1)}, bf16[16,128,128]{2,1,0:T(8,128)(2,1)}, u32[]{:S(2)}, u32[]{:S(2)}) collective-permute-start(bf16[16,128,128]{2,1,0:T(8,128)(2,1)S(1)} %all-to-all-done.1.k0), channel_id=1, source_target_pairs={{0,1},{1,0},{2,3},{3,2},{4,5},{5,4},{6,7},{7,6},{8,9},{9,8},{10,11... | collective-permute-start | bytes 1572872 | tf_op jit(solution)/shard_map/ppermute | solution.py:231
  65.5 24.4 %collective-permute-start.3 = (bf16[16,128,128]{2,1,0:T(8,128)(2,1)}, bf16[16,128,128]{2,1,0:T(8,128)(2,1)S(1)}, u32[]{:S(2)}, u32[]{:S(2)}) collective-permute-start(bf16[16,128,128]{2,1,0:T(8,128)(2,1)} %all-to-all-done.2.v0), channel_id=1, source_target_pairs={{0,1},{1,0},{2,3},{3,2},{4,5},{5,4},{6,7},{7,6},{8,9},{9,8},{10,11... | collective-permute-start | bytes 1572872 | tf_op jit(solution)/shard_map/ppermute | solution.py:231
  77.2 12.7 %collective-permute-start.2 = (bf16[16,128,128]{2,1,0:T(8,128)(2,1)}, bf16[16,128,128]{2,1,0:T(8,128)(2,1)S(1)}, u32[]{:S(2)}, u32[]{:S(2)}) collective-permute-start(bf16[16,128,128]{2,1,0:T(8,128)(2,1)} %collective-permute-done.1.k2), channel_id=1, source_target_pairs={{0,1},{1,0},{2,3},{3,2},{4,5},{5,4},{6,7},{7,6},{8,9},{9,8},{10,11... | collective-permute-start | bytes 1572872 | tf_op jit(solution)/shard_map/ppermute | solution.py:231
  87.3 3.8 %collective-permute-start.5 = (bf16[16,128,128]{2,1,0:T(8,128)(2,1)S(1)}, bf16[16,128,128]{2,1,0:T(8,128)(2,1)S(1)}, u32[]{:S(2)}, u32[]{:S(2)}) collective-permute-start(bf16[16,128,128]{2,1,0:T(8,128)(2,1)S(1)} %collective-permute-done.4.v2), channel_id=1, source_target_pairs={{0,1},{1,0},{2,3},{3,2},{4,5},{5,4},{6,7},{7,6},{8,9},{9,8},{10,11... | collective-permute-start | bytes 1572872 | tf_op jit(solution)/shard_map/ppermute | solution.py:231
  109.0 39.2 %all-to-all-start.3 = ((bf16[16,128,128]{2,1,0:T(8,128)(2,1)}), bf16[16,128,128]{2,1,0:T(8,128)(2,1)S(1)}, u32[]{:S(2)}, u32[]{:S(2)}) async-start(bf16[16,128,128]{2,1,0:T(8,128)(2,1)} %get-tuple-element.4), calls=%async_computation.3 | async-start | bytes 1048576 | tf_op jit(solution)/shard_map/all_to_all | solution.py:228
  122.6 24.3 %copy-start.5 = (s32[20]{0:T(128)S(1)}, s32[20]{0:T(128)}, u32[]{:S(2)}) copy-start(s32[20]{0:T(128)} %hyper_ref.1) | copy-start | bytes 244
  122.6 22.0 %collective-permute-start.6 = (f32[8,128]{1,0:T(8,128)S(1)}, f32[8,128]{1,0:T(8,128)S(1)}, u32[]{:S(2)}, u32[]{:S(2)}) collective-permute-start(f32[8,128]{1,0:T(8,128)S(1)} %own_step.1.own_ref), channel_id=1, source_target_pairs={{64,0},{192,128},{65,1},{193,129},{66,2},{194,130},{67,3},{195,131... | collective-permute-start | bytes 12296 | tf_op jit(solution)/shard_map/ppermute | solution.py:308
  123.9 23.0 %collective-permute-start.7 = (f32[8,128]{1,0:T(8,128)S(1)}, f32[8,128]{1,0:T(8,128)S(1)}, u32[]{:S(2)}, u32[]{:S(2)}) collective-permute-start(f32[8,128]{1,0:T(8,128)S(1)} %own_step.1.own_ref), channel_id=1, source_target_pairs={{128,0},{192,64},{129,1},{193,65},{130,2},{194,66},{131,3},{195,67... | collective-permute-start | bytes 12296 | tf_op jit(solution)/shard_map/ppermute | solution.py:308
  125.2 21.7 %collective-permute-start.8 = (f32[8,128]{1,0:T(8,128)S(1)}, f32[8,128]{1,0:T(8,128)S(1)}, u32[]{:S(2)}, u32[]{:S(2)}) collective-permute-start(f32[8,128]{1,0:T(8,128)S(1)} %own_step.1.own_ref), channel_id=1, source_target_pairs={{0,64},{1,65},{2,66},{3,67},{4,68},{5,69},{6,70},{7,71},{8,72},{9,... | collective-permute-start | bytes 12296 | tf_op jit(solution)/shard_map/ppermute | solution.py:308
  136.1 10.8 %collective-permute-start.9 = (f32[8,128]{1,0:T(8,128)S(1)}, f32[8,128]{1,0:T(8,128)S(1)}, u32[]{:S(2)}, u32[]{:S(2)}) collective-permute-start(f32[8,128]{1,0:T(8,128)S(1)} %own_step.1.own_ref), channel_id=1, source_target_pairs={{0,128},{64,192},{1,129},{65,193},{2,130},{66,194},{3,131},{67,195... | collective-permute-start | bytes 12296 | tf_op jit(solution)/shard_map/ppermute | solution.py:308
  143.9 2.9 %collective-permute-start.10 = (f32[8,128]{1,0:T(8,128)S(1)}, f32[8,128]{1,0:T(8,128)S(1)}, u32[]{:S(2)}, u32[]{:S(2)}) collective-permute-start(f32[8,128]{1,0:T(8,128)S(1)} %own_step.1.own_ref), channel_id=1, source_target_pairs={{128,192},{129,193},{130,194},{131,195},{132,196},{133,197},{134,1... | collective-permute-start | bytes 12296 | tf_op jit(solution)/shard_map/ppermute | solution.py:308
